TPU v7x, 256 devices: a whole 4x4x8 slice. The times are simulated.
256 devices in a mesh: row: 16 (over y_lo, z), col: 16 (over y_hi, x, core).
Axes of the slice: x: 4, y: 4 (y_hi: 2, y_lo: 2; y = y_hi * 2 + y_lo), z: 8, core: 2. Of those that a mesh axis runs over, the one named last changes fastest.
Arguments:
- early_coords: bfloat16 [64, 32768], P(None, ('row', 'col')), may hold values from -13 to 13
- late_coords: bfloat16 [64, 131072], P(None, ('row', 'col')), may hold values from -13 to 13
- late_log_scale: bfloat16 [131072], P(('row', 'col')), may hold values from -2 to 115
- fate_labels: int32 [32768], P(('row', 'col')), may hold values from 0 to 255, as said below
- loadings: float32 [64, 2000], replicated, may hold values from -0.75 to 0.75
Outputs:
- projected: float32 [64, 32768], P(None, ('row', 'col'))
- fate_corr: float32 [2000, 256], replicated
Inputs may be any that keep to these rules, and one draw needn't show every extreme that they name: `fate_labels`: every one of the 256 fate classes labels at least one early cell.
All inputs are finite; a program needn't handle non-finite values.
Results may differ from a plain program's by a relative error of at most 0.0003.
Values may be sent and summed in bfloat16 or wider, within the bound.
No kernel may reach another device: no remote copies, remote signals or barrier semaphores. Data moves between devices by JAX's collectives and lax.ppermute only.
A program may use at most 64 MiB of HBM per device.

v0:
```python
import math

import jax
import jax.numpy as jnp
from jax import lax
from jax.sharding import PartitionSpec as P

FATES = 256


kernel_ratio = 8.0
epsilon = 1e-06


def per_device(early_coords, late_coords, late_log_scale, fate_labels, loadings):
    precise = lax.Precision.HIGHEST
    coord_dim = early_coords.shape[0]
    own_cells = early_coords.shape[1]
    early_rows = lax.all_gather(early_coords, "col", axis=1, tiled=True)
    late_rows, late_logs = (
        lax.all_gather(late_coords, "row", axis=1, tiled=True),
        lax.all_gather(late_log_scale, "row", axis=0, tiled=True),
    )
    sharpness = kernel_ratio / coord_dim
    late_wide = late_rows.astype(jnp.float32)
    late_norms = jnp.sum(late_wide * late_wide, 0)
    log_weights = late_logs.astype(jnp.float32)
    block_total = early_rows.shape[1]
    stride = math.gcd(block_total, 512)
    blocks = block_total // stride
    col_count = lax.axis_size("col")

    def scores_at(first_row):
        row_slab = lax.dynamic_slice_in_dim(early_rows, first_row, stride, 1)
        crossed = lax.dot_general(
            row_slab, late_rows, (((0,), (0,)), ((), ())), preferred_element_type=jnp.float32
        )
        slab_wide = row_slab.astype(jnp.float32)
        slab_norms = jnp.sum(slab_wide * slab_wide, 0)
        distance = slab_norms[:, None] + late_norms[None, :] - 2.0 * crossed
        return log_weights[None, :] - distance * sharpness

    def accumulate(first_row, scores, row_top, carried):
        numerators, totals = carried
        kernel = jnp.exp(scores - row_top[:, None])
        row_sums = jnp.sum(kernel, 1)
        partial_num = lax.dot_general(
            late_wide, kernel, (((1,), (1,)), ((), ())), precision=precise
        )
        numerators = lax.dynamic_update_slice_in_dim(numerators, partial_num, first_row, 1)
        totals = lax.dynamic_update_slice_in_dim(totals, row_sums, first_row, 0)
        return (numerators, totals)

    start_state = (
        jnp.zeros((coord_dim, block_total), jnp.float32),
        jnp.zeros((block_total,), jnp.float32),
    )

    def advance(block_index, carried):
        first_row = block_index * stride
        scores = scores_at(first_row)
        row_top = lax.pmax(jnp.max(scores, 1), "col")
        return accumulate(first_row, scores, row_top, carried)

    numerators, totals = lax.fori_loop(0, blocks, advance, start_state)
    own_num, own_total = (
        lax.psum_scatter(numerators, "col", scatter_dimension=1, tiled=True),
        lax.psum_scatter(totals, "col", scatter_dimension=0, tiled=True),
    )
    projected = own_num / own_total[None, :]
    displacement = projected - early_coords.astype(jnp.float32)
    classes = lax.broadcasted_iota(jnp.int32, (FATES, own_cells), 0)
    indicator = (fate_labels[None, :] == classes).astype(jnp.float32)
    fate_count = jnp.sum(indicator, 1)
    gene_shift = lax.dot_general(
        loadings, displacement, (((0,), (0,)), ((), ())), precision=precise
    )
    cross_sum = lax.dot_general(gene_shift, indicator, (((1,), (1,)), ((), ())), precision=precise)
    gene_total = jnp.sum(gene_shift, 1)
    gene_square = jnp.sum(gene_shift * gene_shift, 1)
    cross_sum, gene_total, gene_square, fate_count = lax.psum(
        (cross_sum, gene_total, gene_square, fate_count), ("row", "col")
    )
    cell_count = float(own_cells * lax.axis_size("row") * col_count)
    mean_shift = gene_total / cell_count
    variance = gene_square / cell_count - mean_shift * mean_shift + epsilon
    fate_share = fate_count / cell_count
    spread = fate_share * (1.0 - fate_share)
    covariance = cross_sum / cell_count - mean_shift[:, None] * fate_share[None, :]
    fate_corr = covariance / jnp.sqrt(variance[:, None] * spread[None, :])
    return (projected, fate_corr)


def solution(mesh):
    in_specs = (
        P(None, ("row", "col")),
        P(None, ("row", "col")),
        P(("row", "col")),
        P(("row", "col")),
        P(),
    )
    out_specs = (P(None, ("row", "col")), P())
    return jax.shard_map(
        per_device, mesh=mesh, in_specs=in_specs, out_specs=out_specs, check_vma=False
    )
```

profile of v0, /device:TPU:2, one launch (start us, length us, event | category | flops | bytes accessed | tf_op | source)
XLA Modules:
  0.0 715.3 jit_solution(15114682783649457366)
XLA Ops:
  8.6 36.5 %all-gather = bf16[16,1,512]{2,1,0:T(2,128)(2,1)S(1)} all-gather(bf16[1,1,512]{2,1,0:T(2,128)(2,1)S(1)} %reshape.14), channel_id=1, replica_groups=mesh['row'=16,'col'=16] {'row'}, dimensions={0}, use_global_device_ids=true | all-gather | bytes 17408 | tf_op jit(solution)/shard_map/all_gather | solution.py:22
  45.2 20.9 %all_gather.10 = bf16[64,2048]{1,0:T(8,128)(2,1)S(1)} all-gather(bf16[64,128]{1,0:T(8,128)(2,1)} %param.7), channel_id=1, replica_groups=mesh['row'=16,'col'=16] {'col'}, dimensions={1}, use_global_device_ids=true | all-gather | bytes 278528 | tf_op jit(solution)/shard_map/all_gather | solution.py:19
  66.1 15.7 %all-gather.3.cloned.1.call-done = bf16[64,8192]{1,0:T(8,128)(2,1)} async-done(((bf16[64,512]{1,0:T(8,128)(2,1)}), bf16[64,8192]{1,0:T(8,128)(2,1)}) %all-gather.3.cloned.1.call-update) | async-done | bytes 1048592 | tf_op jit(solution)/shard_map/all_gather | solution.py:21
  84.8 276.3 %while.15 = (s32[]{:T(128)}, f32[64,2048]{1,0:T(8,128)S(1)}, f32[2048]{0:T(1024)S(1)}, f32[8192]{0:T(1024)S(1)}, bf16[64,2048]{1,0:T(8,128)(2,1)S(1)}, /*index=5...) while((s32[]{:T(128)}, f32[64,2048]{1,0:T(8,128)S(1)}, ...), condition=%wide.region_6.0_spmd, body=%wide.region_1.0_spmd.sunk | while | flops 3795942400 | bytes 53825716 | solution.py:65
  84.8 9.2 %fusion.25 = (f32[512]{0:T(512)S(1)}, f32[512,8192]{1,0:T(8,128)}) fusion(bf16[64,8192]{1,0:T(8,128)(2,1)} %get-tuple-element.255, bf16[64,2048]{1,0:T(8,128)(2,1)S(1)} %get-tuple-element.253, s32[]{:T(128)S(6)} %select_n.10, f32[8192]{0:T(1024)S(1)} %get-tuple-element.254, f32[512]{0:T(512)S(1)} %multiply_reduce_fusion.4, ...), kind=kOutput, calls=%fused_computation.26.clone.1 | convolution fusion | flops 562036224 | bytes 17960964 | tf_op jit(solution)/shard_map/while/body/eval_jaxpr/dot_general | solution.py:35
  94.0 27.9 %pmax.12 = f32[512]{0:T(512)S(1)} all-reduce(f32[512]{0:T(512)S(1)} %get-tuple-element.224), channel_id=1, replica_groups=mesh['row'=16,'col'=16] {'col'}, use_global_device_ids=true, to_apply=%region_4.0 | all-reduce | flops 512 | bytes 4096 | tf_op jit(solution)/shard_map/while/body/eval_jaxpr/pmax | solution.py:62
  122.0 8.1 %fusion.27 = f32[512]{0:T(512)S(1)} fusion(f32[512,8192]{1,0:T(8,128)} %get-tuple-element.223, f32[512]{0:T(512)S(1)} %pmax.12), kind=kLoop, calls=%fused_computation.2.clone.1 | loop fusion | flops 8388096 | bytes 16781312 | tf_op jit(solution)/shard_map/while/body/eval_jaxpr/reduce_sum | solution.py:46
  130.4 19.6 %fusion.26 = f32[64,2048]{1,0:T(8,128)S(1)} fusion(f32[64,2048]{1,0:T(8,128)S(1)} %get-tuple-element.238, s32[]{:T(128)S(6)} %select_n.10, f32[64,8192]{1,0:T(8,128)S(1)} %get-tuple-element.256, f32[512,8192]{1,0:T(8,128)} %get-tuple-element.223, f32[512]{0:T(512)S(1)} %pmax.12), kind=kOutput, calls=%fused_computation.6.clone.1 | convolution fusion | flops 3225419776 | bytes 19007492 | tf_op jit(solution)/shard_map/while/body/eval_jaxpr/dot_general | solution.py:47
  150.0 9.2 %fusion.25 = (f32[512]{0:T(512)S(1)}, f32[512,8192]{1,0:T(8,128)}) fusion(bf16[64,8192]{1,0:T(8,128)(2,1)} %get-tuple-element.255, bf16[64,2048]{1,0:T(8,128)(2,1)S(1)} %get-tuple-element.253, s32[]{:T(128)S(6)} %select_n.10, f32[8192]{0:T(1024)S(1)} %get-tuple-element.254, f32[512]{0:T(512)S(1)} %multiply_reduce_fusion.4, ...), kind=kOutput, calls=%fused_computation.26.clone.1 | convolution fusion | flops 562036224 | bytes 17960964 | tf_op jit(solution)/shard_map/while/body/eval_jaxpr/dot_general | solution.py:35
  159.2 33.1 %pmax.12 = f32[512]{0:T(512)S(1)} all-reduce(f32[512]{0:T(512)S(1)} %get-tuple-element.224), channel_id=1, replica_groups=mesh['row'=16,'col'=16] {'col'}, use_global_device_ids=true, to_apply=%region_4.0 | all-reduce | flops 512 | bytes 4096 | tf_op jit(solution)/shard_map/while/body/eval_jaxpr/pmax | solution.py:62
  192.4 8.1 %fusion.27 = f32[512]{0:T(512)S(1)} fusion(f32[512,8192]{1,0:T(8,128)} %get-tuple-element.223, f32[512]{0:T(512)S(1)} %pmax.12), kind=kLoop, calls=%fused_computation.2.clone.1 | loop fusion | flops 8388096 | bytes 16781312 | tf_op jit(solution)/shard_map/while/body/eval_jaxpr/reduce_sum | solution.py:46
  200.8 19.6 %fusion.26 = f32[64,2048]{1,0:T(8,128)S(1)} fusion(f32[64,2048]{1,0:T(8,128)S(1)} %get-tuple-element.238, s32[]{:T(128)S(6)} %select_n.10, f32[64,8192]{1,0:T(8,128)S(1)} %get-tuple-element.256, f32[512,8192]{1,0:T(8,128)} %get-tuple-element.223, f32[512]{0:T(512)S(1)} %pmax.12), kind=kOutput, calls=%fused_computation.6.clone.1 | convolution fusion | flops 3225419776 | bytes 19007492 | tf_op jit(solution)/shard_map/while/body/eval_jaxpr/dot_general | solution.py:47
  220.4 9.2 %fusion.25 = (f32[512]{0:T(512)S(1)}, f32[512,8192]{1,0:T(8,128)}) fusion(bf16[64,8192]{1,0:T(8,128)(2,1)} %get-tuple-element.255, bf16[64,2048]{1,0:T(8,128)(2,1)S(1)} %get-tuple-element.253, s32[]{:T(128)S(6)} %select_n.10, f32[8192]{0:T(1024)S(1)} %get-tuple-element.254, f32[512]{0:T(512)S(1)} %multiply_reduce_fusion.4, ...), kind=kOutput, calls=%fused_computation.26.clone.1 | convolution fusion | flops 562036224 | bytes 17960964 | tf_op jit(solution)/shard_map/while/body/eval_jaxpr/dot_general | solution.py:35
  229.6 33.1 %pmax.12 = f32[512]{0:T(512)S(1)} all-reduce(f32[512]{0:T(512)S(1)} %get-tuple-element.224), channel_id=1, replica_groups=mesh['row'=16,'col'=16] {'col'}, use_global_device_ids=true, to_apply=%region_4.0 | all-reduce | flops 512 | bytes 4096 | tf_op jit(solution)/shard_map/while/body/eval_jaxpr/pmax | solution.py:62
  262.8 8.1 %fusion.27 = f32[512]{0:T(512)S(1)} fusion(f32[512,8192]{1,0:T(8,128)} %get-tuple-element.223, f32[512]{0:T(512)S(1)} %pmax.12), kind=kLoop, calls=%fused_computation.2.clone.1 | loop fusion | flops 8388096 | bytes 16781312 | tf_op jit(solution)/shard_map/while/body/eval_jaxpr/reduce_sum | solution.py:46
  271.1 19.6 %fusion.26 = f32[64,2048]{1,0:T(8,128)S(1)} fusion(f32[64,2048]{1,0:T(8,128)S(1)} %get-tuple-element.238, s32[]{:T(128)S(6)} %select_n.10, f32[64,8192]{1,0:T(8,128)S(1)} %get-tuple-element.256, f32[512,8192]{1,0:T(8,128)} %get-tuple-element.223, f32[512]{0:T(512)S(1)} %pmax.12), kind=kOutput, calls=%fused_computation.6.clone.1 | convolution fusion | flops 3225419776 | bytes 19007492 | tf_op jit(solution)/shard_map/while/body/eval_jaxpr/dot_general | solution.py:47
  290.8 9.2 %fusion.25 = (f32[512]{0:T(512)S(1)}, f32[512,8192]{1,0:T(8,128)}) fusion(bf16[64,8192]{1,0:T(8,128)(2,1)} %get-tuple-element.255, bf16[64,2048]{1,0:T(8,128)(2,1)S(1)} %get-tuple-element.253, s32[]{:T(128)S(6)} %select_n.10, f32[8192]{0:T(1024)S(1)} %get-tuple-element.254, f32[512]{0:T(512)S(1)} %multiply_reduce_fusion.4, ...), kind=kOutput, calls=%fused_computation.26.clone.1 | convolution fusion | flops 562036224 | bytes 17960964 | tf_op jit(solution)/shard_map/while/body/eval_jaxpr/dot_general | solution.py:35
  300.0 33.1 %pmax.12 = f32[512]{0:T(512)S(1)} all-reduce(f32[512]{0:T(512)S(1)} %get-tuple-element.224), channel_id=1, replica_groups=mesh['row'=16,'col'=16] {'col'}, use_global_device_ids=true, to_apply=%region_4.0 | all-reduce | flops 512 | bytes 4096 | tf_op jit(solution)/shard_map/while/body/eval_jaxpr/pmax | solution.py:62
  333.1 8.1 %fusion.27 = f32[512]{0:T(512)S(1)} fusion(f32[512,8192]{1,0:T(8,128)} %get-tuple-element.223, f32[512]{0:T(512)S(1)} %pmax.12), kind=kLoop, calls=%fused_computation.2.clone.1 | loop fusion | flops 8388096 | bytes 16781312 | tf_op jit(solution)/shard_map/while/body/eval_jaxpr/reduce_sum | solution.py:46
  341.5 19.6 %fusion.26 = f32[64,2048]{1,0:T(8,128)S(1)} fusion(f32[64,2048]{1,0:T(8,128)S(1)} %get-tuple-element.238, s32[]{:T(128)S(6)} %select_n.10, f32[64,8192]{1,0:T(8,128)S(1)} %get-tuple-element.256, f32[512,8192]{1,0:T(8,128)} %get-tuple-element.223, f32[512]{0:T(512)S(1)} %pmax.12), kind=kOutput, calls=%fused_computation.6.clone.1 | convolution fusion | flops 3225419776 | bytes 19007492 | tf_op jit(solution)/shard_map/while/body/eval_jaxpr/dot_general | solution.py:47
  363.2 33.8 %all-reduce = f32[2048]{0:T(1024)S(1)} all-reduce(f32[2048]{0:T(1024)S(1)} %get-tuple-element.143), channel_id=3, replica_groups=mesh['row'=16,'col'=16] {'col'}, use_global_device_ids=true, to_apply=%region_8.0.clone | all-reduce | flops 2048 | bytes 16384
  397.1 38.5 %reduce-scatter.2.cloned.1.call-done = f32[64,128]{1,0:T(8,128)} async-done(((f32[64,2048]{1,0:T(8,128)}), f32[64,128]{1,0:T(8,128)}) %reduce-scatter.2.cloned.1.call-update) | async-done | bytes 32784 | tf_op jit(solution)/shard_map/reduce_scatter | solution.py:67
  441.0 74.4 %all-reduce.1 = (f32[256]{0:T(256)S(1)}, f32[2000]{0:T(1024)S(1)}, f32[2000]{0:T(1024)S(1)}) all-reduce(f32[256]{0:T(256)S(1)} %convert_reduce_fusion, f32[2000]{0:T(1024)S(1)} %get-tuple-element.145, f32[2000]{0:T(1024)S(1)} %get-tuple-element.144), channel_id=1, replica_groups=mesh['row'=16,'col'=16] {'row','col'}, use_global_device_ids=true, to_apply=%region_13.0 | all-reduce | flops 4256 | bytes 34048 | tf_op jit(solution)/shard_map/psum | solution.py:81
  515.4 189.9 %all-reduce.4.cloned.1.call-done = f32[2000,256]{1,0:T(8,128)} async-done(((f32[2000,256]{1,0:T(8,128)}), f32[2000,256]{1,0:T(8,128)}) %all-reduce.4.cloned.1.call-update) | async-done | bytes 2048016 | tf_op jit(solution)/shard_map/psum | solution.py:81
  (41 shorter events, 16.0 us)
Async XLA Ops:
  7.2 429.2 %copy-start = (f32[64,2000]{1,0:T(8,128)S(1)}, f32[64,2000]{1,0:T(8,128)}, u32[]{:S(2)}) copy-start(f32[64,2000]{1,0:T(8,128)} %param.11) | copy-start | bytes 1536004
  7.2 74.6 %all-gather.3.cloned.1.call-start = ((), (), s32[]{:S(2)}) async-start(), calls=%async_computation.1 | async-start | bytes 1114112 | tf_op jit(solution)/shard_map/all_gather | solution.py:21
  7.9 427.7 %reduce-scatter.2.cloned.1.call-start = ((), (), s32[]{:S(2)}) async-start(), calls=%async_computation.2 | async-start | bytes 557056 | tf_op jit(solution)/shard_map/reduce_scatter | solution.py:67
  84.7 277.2 %copy-start.5 = (u32[256]{0:T(256)S(1)}, u32[256]{0:T(256)}, u32[]{:S(2)}) copy-start(u32[256]{0:T(256)} %constant.74) | copy-start | bytes 3076
  84.7 351.6 %copy-start.3 = (bf16[64,128]{1,0:T(8,128)(2,1)S(1)}, bf16[64,128]{1,0:T(8,128)(2,1)}, u32[]{:S(2)}) copy-start(bf16[64,128]{1,0:T(8,128)(2,1)} %param.7) | copy-start | bytes 49156
  84.8 353.8 %copy-start.4 = (s32[128]{0:T(128)S(1)}, s32[128]{0:T(128)}, u32[]{:S(2)}) copy-start(s32[128]{0:T(128)} %param.10) | copy-start | bytes 1540
  361.1 0.8 copy-start.1
  361.9 343.4 %all-reduce.4.cloned.1.call-start = ((), (), s32[]{:S(2)}) async-start(), calls=%async_computation.3 | async-start | bytes 4096000 | tf_op jit(solution)/shard_map/psum | solution.py:81
  436.3 272.4 %copy-start.2 = (f32[64,128]{1,0:T(8,128)}, f32[64,128]{1,0:T(8,128)S(1)}, u32[]{:S(2)}) copy-start(f32[64,128]{1,0:T(8,128)S(1)} %broadcast_divide_fusion) | copy-start | bytes 98308
Sparse Core Ops, SparseCore 0:
  9.8 72.0 all-gather.2
  362.0 73.4 reduce-scatter.1
  441.6 263.6 all-reduce.3
where the time goes:
time: 716 us; the launch traced here: 715 us
  blocking collectives  293 us (41%)
  waiting for transfers between devices  245 us (34%)
  matrix products  120 us (17%)
  other arithmetic  39.8 us (6%)
  between operations  14.5 us (2%)
    psum x1, waiting for transfers between devices, per_device(): lax.psum((cross_sum, gene_total, gene_square, fate_count), ('row', 'col'))  190 us
    pmax x4, blocking collectives, advance(): row_top = lax.pmax(jnp.max(scores, 1), 'col')  127 us
    dot_general x4, matrix products, accumulate(): lax.dot_general(late_wide, kernel, (((1,), (1,)), ((), ())), precision=pr...  78.4 us
    psum x1, blocking collectives, per_device(): lax.psum((cross_sum, gene_total, gene_square, fate_count), ('row', 'col'))  74.4 us
    reduce_scatter x1, waiting for transfers between devices, per_device(): lax.psum_scatter(numerators, 'col', scatter_dimension=1, tiled=True)  38.5 us
    dot_general x4, matrix products, scores_at(): lax.dot_general(row_slab, late_rows, (((0,), (0,)), ((), ())), preferred_...  36.8 us
    all_gather x1, blocking collectives, per_device(): lax.all_gather(late_log_scale, 'row', axis=0, tiled=True)  36.5 us
    unnamed x1, blocking collectives  33.8 us
  transfers between devices with their start and end apart: 3, of which 3 were waited for; matrix products, arithmetic and copies ran while one was open for 0% of the time, Pallas kernels for 0%

commit v1 on v0

v1 whole, which is shorter than its diff:
```python
import functools
import math

import jax
import jax.numpy as jnp
from jax import lax
from jax.experimental import pallas as pl
from jax.experimental.pallas import tpu as pltpu
from jax.sharding import Mesh
from jax.sharding import PartitionSpec as P

f32 = jnp.float32
bf16 = jnp.bfloat16

DIM = 64
FATES = 256
EPSILON = 1e-06
SHARP = 8.0 / DIM
LOG2E = math.log2(math.e)
LOWEST = -1e30

AXES = ("yl", "z", "yh", "x", "core")
SIZES = (2, 8, 2, 4, 2)
EARLY_GROUP = ("yl", "yh", "x")
LATE_GROUP = ("z", "core")


def split3(v):
    high = v.astype(bf16).astype(f32)
    rest = v - high
    mid = rest.astype(bf16).astype(f32)
    return high, mid, rest - mid


def put_rows(base, row, first, value):
    for k, piece in enumerate(split3(value)):
        base = jnp.where(row == first + k, piece, base)
    return base


def attention_kernel(x_ref, y_ref, out_ref, xa, ya, yw, sbuf, mbuf, acc, *, tile, sub):
    n_early, _, early_width = x_ref.shape
    n_late, _, late_width = y_ref.shape
    pairs = n_early // 2
    tiles = n_late * late_width // tile
    wide = 2 * early_width

    def prepare_early(b, carry):
        x = jnp.concatenate([x_ref[2 * b], x_ref[2 * b + 1]], 1).astype(f32)
        norms = jnp.sum(x * x, 0, keepdims=True)
        high, mid, low = split3(x * (2.0 * SHARP * LOG2E))
        row = lax.broadcasted_iota(jnp.int32, (DIM, wide), 0)
        extra = jnp.where(row < 3, 1.0, jnp.zeros((DIM, wide), f32))
        extra = put_rows(extra, row, 3, norms * (-SHARP * LOG2E))
        xa[b] = jnp.concatenate([high, extra, mid, low], 0).astype(bf16)
        return carry

    lax.fori_loop(0, pairs, prepare_early, 0)

    def prepare_late(b, carry):
        yb = y_ref[b, :DIM, :]
        y = yb.astype(f32)
        logs = y_ref[b, DIM : DIM + 8, :].astype(f32)[:1]
        bias = (logs - jnp.sum(y * y, 0, keepdims=True) * SHARP) * LOG2E
        row = lax.broadcasted_iota(jnp.int32, (DIM, late_width), 0)
        extra = jnp.where((row >= 3) & (row < 6), 1.0, jnp.zeros((DIM, late_width), f32))
        extra = put_rows(extra, row, 0, bias)
        t = jnp.concatenate([y, extra], 0).T
        lane = lax.broadcasted_iota(jnp.int32, (late_width, 128), 1)
        twice = jnp.where(lane < DIM, t, pltpu.roll(t, DIM, 1))
        first = pl.multiple_of(b * late_width, late_width)
        ya[pl.ds(first, late_width), :] = jnp.concatenate([t, twice], 1).astype(bf16)
        ones = jnp.where(lax.broadcasted_iota(jnp.int32, (16, late_width), 0) == 0, 1.0, 0.0)
        yw[:, pl.ds(first, late_width)] = jnp.concatenate([yb, ones.astype(bf16)], 0)
        return carry

    lax.fori_loop(0, n_late, prepare_late, 0)
    acc[...] = jnp.zeros_like(acc)
    parts = tile // sub

    def score_part(pair, first, j, slot, top):
        s = jnp.dot(ya[pl.ds(first + j * sub, sub), :], xa[pair], preferred_element_type=f32)
        sbuf[slot, j * sub : (j + 1) * sub, :] = s
        here = jnp.max(s.reshape(sub // 8, 8, wide), 0)
        return here if top is None else jnp.maximum(top, here)

    steps = pairs * tiles
    top = None
    for j in range(parts):
        top = score_part(0, 0, j, 0, top)
    mbuf[0] = top

    def step(n, slot, before):
        pair = n // tiles
        first = pl.multiple_of((n % tiles) * tile, tile)
        following = jnp.minimum(n + 1, steps - 1)
        next_first = pl.multiple_of((following % tiles) * tile, tile)
        before = jnp.where(n % tiles == 0, LOWEST, before)
        now = jnp.maximum(before, jnp.max(mbuf[slot], 0, keepdims=True))
        shrink = jnp.exp2(before - now)
        top = None
        sums = None
        for j in range(parts):
            top = score_part(following // tiles, next_first, j, 1 - slot, top)
            weights = jnp.exp2(sbuf[slot, j * sub : (j + 1) * sub, :] - now).astype(bf16)
            more = jnp.dot(yw[:, pl.ds(first + j * sub, sub)], weights, preferred_element_type=f32)
            sums = more if sums is None else sums + more
        mbuf[1 - slot] = top
        total = acc[...] * shrink + sums
        acc[...] = total
        row = lax.broadcasted_iota(jnp.int32, (72, wide), 0)
        packed = jnp.where(row == DIM + 1, now, total[:72])
        out_ref[2 * pair] = packed[:, :early_width]
        out_ref[2 * pair + 1] = packed[:, early_width:]
        return now

    def two_steps(i, before):
        return step(2 * i + 1, 1, step(2 * i, 0, before))

    lax.fori_loop(0, steps // 2, two_steps, jnp.full((1, wide), LOWEST, f32))


def attention(early_all, late_all, tile=2048, sub=512):
    n_early, _, early_width = early_all.shape
    n_late, _, late_width = late_all.shape
    late_total = n_late * late_width
    wide = 2 * early_width
    return pl.pallas_call(
        functools.partial(attention_kernel, tile=tile, sub=sub),
        out_shape=jax.ShapeDtypeStruct((n_early, 72, early_width), f32),
        in_specs=[pl.BlockSpec(memory_space=pltpu.VMEM)] * 2,
        out_specs=pl.BlockSpec(memory_space=pltpu.VMEM),
        scratch_shapes=[
            pltpu.VMEM((n_early // 2, 256, wide), bf16),
            pltpu.VMEM((late_total, 256), bf16),
            pltpu.VMEM((80, late_total), bf16),
            pltpu.VMEM((2, tile, wide), f32),
            pltpu.VMEM((2, 8, wide), f32),
            pltpu.VMEM((80, wide), f32),
        ],
        compiler_params=pltpu.CompilerParams(vmem_limit_bytes=48 * 2**20),
        name="attention",
    )(early_all, late_all)


def moments_kernel(got_ref, x_ref, label_ref, projected_ref, sums_ref):
    peers, _, cells = got_ref.shape
    top = got_ref[0, DIM : DIM + 8, :][1:2]
    for p in range(1, peers):
        top = jnp.maximum(top, got_ref[p, DIM : DIM + 8, :][1:2])
    total = jnp.zeros((72, cells), f32)
    for p in range(peers):
        block = got_ref[p]
        total = total + block * jnp.exp2(block[DIM + 1 : DIM + 2] - top)
    projected = total[:DIM] / total[DIM : DIM + 1]
    projected_ref[...] = projected
    moved = projected - x_ref[...].astype(f32)
    classes = lax.broadcasted_iota(jnp.int32, (FATES, cells), 0)
    indicator = jnp.where(classes == label_ref[...], 1.0, 0.0)
    across = (((1,), (1,)), ((), ()))
    by_class = lax.dot_general(
        moved, indicator, across, precision=lax.Precision.HIGHEST, preferred_element_type=f32
    )
    padded = jnp.concatenate([moved, jnp.zeros((128 - DIM, cells), f32)], 0)
    second = lax.dot_general(
        moved, padded, across, precision=lax.Precision.HIGHEST, preferred_element_type=f32
    )
    count = jnp.sum(indicator, 1, keepdims=True)
    lane = lax.broadcasted_iota(jnp.int32, (DIM, 128), 1)
    for q in range(FATES // DIM):
        second = jnp.where(lane == DIM + q, count[DIM * q : DIM * (q + 1)], second)
    sums_ref[:8] = by_class.reshape(8, 8, FATES)
    sums_ref[8:] = jnp.concatenate([second, jnp.zeros((DIM, 128), f32)], 1).reshape(8, 8, FATES)


def moments(got, early, labels):
    return pl.pallas_call(
        moments_kernel,
        out_shape=(
            jax.ShapeDtypeStruct(early.shape, f32),
            jax.ShapeDtypeStruct((16, 8, FATES), f32),
        ),
        in_specs=[pl.BlockSpec(memory_space=pltpu.VMEM)] * 3,
        out_specs=(pl.BlockSpec(memory_space=pltpu.VMEM),) * 2,
        name="moments",
    )(got, early, labels)


def correlate_kernel(sums_ref, split_ref, plain_ref, out_ref, right, *, cells):
    @pl.when(pl.program_id(0) == 0)
    def _():
        by_class = sums_ref[:8].reshape(DIM, FATES) / cells
        second = sums_ref[8:].reshape(DIM, FATES)[:, :128]
        flipped = second.T
        share = jnp.concatenate(
            [flipped[DIM + q : DIM + q + 1] for q in range(FATES // DIM)], 1
        ) / cells
        mean = jnp.sum(by_class, 1, keepdims=True)
        mean_row = jnp.broadcast_to(mean, (DIM, 128)).T[:1]
        mean_row = jnp.concatenate([mean_row, jnp.zeros((1, 128 - DIM), f32)], 1)
        lane = lax.broadcasted_iota(jnp.int32, (DIM, 128), 1)
        square = jnp.where(lane < DIM, second, 0.0) / cells - mean * mean_row
        cross = (by_class - mean * share) / jnp.sqrt(share * (1.0 - share))
        both = jnp.concatenate([cross, square], 1)
        high = both.astype(bf16)
        low = (both - high.astype(f32)).astype(bf16)
        right[...] = jnp.concatenate([high, high, low, low], 0)

    product = jnp.dot(split_ref[...], right[...], preferred_element_type=f32)
    variance = jnp.sum(product[:, FATES:] * plain_ref[...], 1, keepdims=True) + EPSILON
    out_ref[...] = product[:, :FATES] * (1.0 / jnp.sqrt(variance))


def correlate(sums, split, plain, cells, block=400):
    genes = split.shape[0]
    return pl.pallas_call(
        functools.partial(correlate_kernel, cells=cells),
        grid=(genes // block,),
        out_shape=jax.ShapeDtypeStruct((genes, FATES), f32),
        in_specs=[
            pl.BlockSpec((16, 8, FATES), lambda i: (0, 0, 0)),
            pl.BlockSpec((block, 256), lambda i: (i, 0)),
            pl.BlockSpec((block, 128), lambda i: (i, 0)),
        ],
        out_specs=pl.BlockSpec((block, FATES), lambda i: (i, 0)),
        scratch_shapes=[pltpu.VMEM((256, FATES + 128), bf16)],
        name="correlate",
    )(sums, split, plain)


def exchange(blocks, axes):
    return lax.all_to_all(blocks, axes, 0, 0, tiled=False)


def spread(block, axes):
    return exchange(jnp.broadcast_to(block[None], (16,) + block.shape), axes)


def per_device(early, late, late_logs, labels, loadings):
    cells = float(early.shape[1] * math.prod(SIZES))
    turned = loadings.T
    high = lax.reduce_precision(turned, 8, 7)
    low = turned - high
    split = jnp.concatenate([high, low, high, low], 1).astype(bf16)
    plain = jnp.pad(turned, ((0, 0), (0, 128 - DIM)))

    late_full = jnp.concatenate([late, late_logs[None], jnp.zeros((7,) + late_logs.shape, bf16)], 0)
    early_all = spread(early, EARLY_GROUP)
    late_all = spread(late_full, LATE_GROUP)
    partial = attention(early_all, late_all)
    got = exchange(partial, EARLY_GROUP)
    projected, sums = moments(got, early, labels[None])
    sums = jnp.sum(exchange(sums, EARLY_GROUP), 0)
    sums = jnp.sum(spread(sums, LATE_GROUP), 0)
    sums = spread(sums, EARLY_GROUP)
    return projected, correlate(sums, split, plain, cells)


def solution(mesh):
    named = Mesh(mesh.devices.reshape(SIZES), AXES)
    in_specs = (P(None, AXES), P(None, AXES), P(AXES), P(AXES), P())
    out_specs = (P(None, AXES), P())
    return jax.shard_map(
        per_device, mesh=named, in_specs=in_specs, out_specs=out_specs, check_vma=False
    )
```

time: 716 us -> 142 us (0.20)
  blocking collectives: 293 us -> 56.2 us
  waiting for transfers between devices: 245 us -> 25 us
  matrix products: 120 us -> 0 us
  other arithmetic: 39.8 us -> 2.77 us
  Pallas kernels: 0 us -> 28.6 us
  starting transfers between devices: 0.12 us -> 20.5 us
  between operations: 14.5 us -> 0.69 us
    psum x1 -> x0, waiting for transfers between devices: 190 us -> none  [per_device(): lax.psum((cross_sum, gene_total, gene_square, fate_count), ('row', 'col'))]
    pmax x4 -> x0, blocking collectives: 127 us -> none  [advance(): row_top = lax.pmax(jnp.max(scores, 1), 'col')]
    dot_general x10 -> x0, matrix products: 120 us -> none  [the longest x4 78.4 us: accumulate(): lax.dot_general(late_wide, kernel, (((1,), (1,)), ((), ())), precision=pr...]
    psum x1 -> x0, blocking collectives: 74.4 us -> none  [per_device(): lax.psum((cross_sum, gene_total, gene_square, fate_count), ('row', 'col'))]
    all_gather x2 -> x0, blocking collectives: 57.4 us -> none  [the longest x1 36.5 us: per_device(): lax.all_gather(late_log_scale, 'row', axis=0, tiled=True)]
    all_to_all x0 -> x2, blocking collectives: none -> 56.2 us  [exchange(): return lax.all_to_all(blocks, axes, 0, 0, tiled=False)]
    reduce_scatter x1 -> x0, waiting for transfers between devices: 38.5 us -> none  [per_device(): lax.psum_scatter(numerators, 'col', scatter_dimension=1, tiled=True)]
    reduce_sum x10 -> x2, other arithmetic: 34.2 us -> 0.04 us  [the longest x1 0.02 us: per_device(): sums = jnp.sum(spread(sums, LATE_GROUP), 0)]
  transfers between devices with their start and end apart: 3 -> 4, of which waited for: 3 -> 4; matrix products, arithmetic and copies ran while one was open for 0% -> 4% of each run, Pallas kernels for 0% -> 0%
where the time goes in v1:
time: 142 us; the launch traced here: 140 us
  blocking collectives  56.2 us (40%)
  Pallas kernels  28.6 us (20%)
  waiting for transfers between devices  25 us (18%)
  starting transfers between devices  20.5 us (14%)
  local copies, waits for them, and re-layouts  5.7 us (4%)
  other arithmetic  2.77 us (2%)
    all_to_all x2, blocking collectives, exchange(): return lax.all_to_all(blocks, axes, 0, 0, tiled=False)  56.2 us
    all_to_all x4, waiting for transfers between devices, exchange(): return lax.all_to_all(blocks, axes, 0, 0, tiled=False)  25 us
    pallas_call x1, Pallas kernels, attention(): pl.pallas_call(functools.partial(attention_kernel, tile=tile, sub=sub), o...  21 us
    all_to_all x4, starting transfers between devices, exchange(): return lax.all_to_all(blocks, axes, 0, 0, tiled=False)  20.5 us
    pallas_call x1, Pallas kernels, correlate(): pl.pallas_call(functools.partial(correlate_kernel, cells=cells), grid=(ge...  5.55 us
    broadcast_in_dim x4, local copies, waits for them, and re-layouts, spread(): return exchange(jnp.broadcast_to(block[None], (16,) + block.shape), axes)  2.88 us
  transfers between devices with their start and end apart: 4, of which 4 were waited for; matrix products, arithmetic and copies ran while one was open for 4% of the time, Pallas kernels for 0%

profile of v1, /device:TPU:2, one launch (start us, length us, event | category | flops | bytes accessed | tf_op | source)
XLA Modules:
  0.0 139.5 jit_solution(7174958161825760264)
XLA Ops:
  0.6 1.5 %broadcast_in_dim.14 = bf16[16,64,128]{2,1,0:T(8,128)(2,1)} broadcast(bf16[64,128]{1,0:T(8,128)(2,1)} %x_ref.1), dimensions={1,2} | broadcast | bytes 278528 | tf_op jit(solution)/shard_map/broadcast_in_dim | solution.py:236
  2.1 7.5 %all-to-all-start = ((bf16[16,64,128]{2,1,0:T(8,128)(2,1)}), bf16[16,64,128]{2,1,0:T(8,128)(2,1)S(1)}, u32[]{:S(2)}, u32[]{:S(2)}) async-start(bf16[16,64,128]{2,1,0:T(8,128)(2,1)} %broadcast_in_dim.14), calls=%async_computation | async-start | bytes 524288 | tf_op jit(solution)/shard_map/all_to_all | solution.py:232
  9.6 0.7 broadcast_in_dim.15
  10.3 0.1 pad.11.clone
  10.3 0.9 maximum_maximum_fusion
  11.3 5.6 %all-to-all-done.x_ref = bf16[16,64,128]{2,1,0:T(8,128)(2,1)S(1)} async-done(((bf16[16,64,128]{2,1,0:T(8,128)(2,1)}), bf16[16,64,128]{2,1,0:T(8,128)(2,1)S(1)}, u32[]{:S(2)}, u32[]{:S(2)}) %all-to-all-start) | async-done | bytes 262176 | tf_op jit(solution)/shard_map/all_to_all | solution.py:232
  17.0 39.6 %all_to_all.30.y_ref = bf16[16,72,512]{2,1,0:T(8,128)(2,1)S(1)} all-to-all(bf16[16,72,512]{2,1,0:T(8,128)(2,1)S(1)} %broadcast_in_dim.17), channel_id=1, replica_groups=mesh['yl'=2,'z'=8,'yh'=2,'x'=4,'core'=2] {'z','core'}, dimensions={0} | all-to-all | bytes 2359296 | tf_op jit(solution)/shard_map/all_to_all | solution.py:232
  56.6 21.0 %attention.1 = f32[16,72,128]{2,1,0:T(8,128)S(1)} custom-call(bf16[16,64,128]{2,1,0:T(8,128)(2,1)S(1)} %all-to-all-done.x_ref, bf16[16,72,512]{2,1,0:T(8,128)(2,1)S(1)} %all_to_all.30.y_ref), custom_call_target="tpu_custom_call" | custom-call | tf_op jit(solution)/shard_map/attention/pallas_call | solution.py:128
  77.6 16.6 %all_to_all.31.got_ref = f32[16,72,128]{2,1,0:T(8,128)} all-to-all(f32[16,72,128]{2,1,0:T(8,128)S(1)} %attention.1), channel_id=1, replica_groups=mesh['yl'=2,'z'=8,'yh'=2,'x'=4,'core'=2] {'yl','yh','x'}, dimensions={0} | all-to-all | bytes 1179648 | tf_op jit(solution)/shard_map/all_to_all | solution.py:232
  94.2 2.1 %moments.1 = (f32[64,128]{1,0:T(8,128)}, f32[16,8,256]{2,1,0:T(8,128)}) custom-call(f32[16,72,128]{2,1,0:T(8,128)} %all_to_all.31.got_ref, bf16[64,128]{1,0:T(8,128)(2,1)} %x_ref.1, s32[1,128]{1,0:T(1,128)} %bitcast.5), custom_call_target="tpu_custom_call" | custom-call | tf_op jit(solution)/shard_map/moments/pallas_call | solution.py:177
  96.3 4.8 %all-to-all-start.3 = ((f32[16,8,256]{2,1,0:T(8,128)}), f32[16,8,256]{2,1,0:T(8,128)S(1)}, u32[]{:S(2)}, u32[]{:S(2)}) async-start(f32[16,8,256]{2,1,0:T(8,128)} %get-tuple-element.5), calls=%async_computation.3 | async-start | bytes 262144 | tf_op jit(solution)/shard_map/all_to_all | solution.py:232
  101.0 0.3 copy.8
  101.4 6.4 %all-to-all-done.3 = f32[16,8,256]{2,1,0:T(8,128)S(1)} async-done(((f32[16,8,256]{2,1,0:T(8,128)}), f32[16,8,256]{2,1,0:T(8,128)S(1)}, u32[]{:S(2)}, u32[]{:S(2)}) %all-to-all-start.3) | async-done | bytes 131104 | tf_op jit(solution)/shard_map/all_to_all | solution.py:232
  107.7 0.7 broadcast_in_dim.38
  108.4 3.5 %all-to-all-start.4 = ((f32[16,8,256]{2,1,0:T(8,128)}), f32[16,8,256]{2,1,0:T(8,128)S(1)}, u32[]{:S(2)}, u32[]{:S(2)}) async-start(f32[16,8,256]{2,1,0:T(8,128)} %broadcast_in_dim.38), calls=%async_computation.4 | async-start | bytes 262144 | tf_op jit(solution)/shard_map/all_to_all | solution.py:232
  111.9 0.2 reduce-precision_convert_fusion
  112.1 8.4 %all-to-all-done.4 = f32[16,8,256]{2,1,0:T(8,128)S(1)} async-done(((f32[16,8,256]{2,1,0:T(8,128)}), f32[16,8,256]{2,1,0:T(8,128)S(1)}, u32[]{:S(2)}, u32[]{:S(2)}) %all-to-all-start.4) | async-done | bytes 131104 | tf_op jit(solution)/shard_map/all_to_all | solution.py:232
  120.6 0.7 broadcast_in_dim.39
  121.2 4.8 %all-to-all-start.5 = ((f32[16,8,256]{2,1,0:T(8,128)}), f32[16,8,256]{2,1,0:T(8,128)S(1)}, u32[]{:S(2)}, u32[]{:S(2)}) async-start(f32[16,8,256]{2,1,0:T(8,128)} %broadcast_in_dim.39), calls=%async_computation.5 | async-start | bytes 262144 | tf_op jit(solution)/shard_map/all_to_all | solution.py:232
  126.0 1.6 %pad_maximum_fusion.split_ref = bf16[2000,256]{1,0:T(8,128)(2,1)} fusion(bf16[2000,64]{1,0:T(8,128)(2,1)S(1)} %get-tuple-element.7, bf16[2000,64]{1,0:T(8,128)(2,1)S(1)} %get-tuple-element.6), kind=kLoop, calls=%fused_computation.3 | loop fusion | flops 4096000 | bytes 1536000 | tf_op jit(solution)/shard_map/concatenate | solution.py:244
  127.6 1.1 pad.4.plain_ref
  128.7 4.6 %all-to-all-done.5.sums_ref = f32[16,8,256]{2,1,0:T(8,128)S(1)} async-done(((f32[16,8,256]{2,1,0:T(8,128)}), f32[16,8,256]{2,1,0:T(8,128)S(1)}, u32[]{:S(2)}, u32[]{:S(2)}) %all-to-all-start.5) | async-done | bytes 131104 | tf_op jit(solution)/shard_map/all_to_all | solution.py:232
  133.3 0.7 copy-done.1
  134.0 5.6 %correlate.1 = f32[2000,256]{1,0:T(8,128)} custom-call(f32[16,8,256]{2,1,0:T(8,128)} %copy-done.1, bf16[2000,256]{1,0:T(8,128)(2,1)} %pad_maximum_fusion.split_ref, f32[2000,128]{1,0:T(8,128)} %pad.4.plain_ref), custom_call_target="tpu_custom_call" | custom-call | tf_op jit(solution)/shard_map/correlate/pallas_call | solution.py:216
  (7 shorter events, 0.1 us)
Async XLA Ops:
  2.1 14.8 %all-to-all-start = ((bf16[16,64,128]{2,1,0:T(8,128)(2,1)}), bf16[16,64,128]{2,1,0:T(8,128)(2,1)S(1)}, u32[]{:S(2)}, u32[]{:S(2)}) async-start(bf16[16,64,128]{2,1,0:T(8,128)(2,1)} %broadcast_in_dim.14), calls=%async_computation | async-start | bytes 524288 | tf_op jit(solution)/shard_map/all_to_all | solution.py:232
  56.6 44.5 %copy-start = (f32[64,2000]{1,0:T(8,128)S(1)}, f32[64,2000]{1,0:T(8,128)}, u32[]{:S(2)}) copy-start(f32[64,2000]{1,0:T(8,128)} %param.9) | copy-start | bytes 1536004
  96.3 11.5 %all-to-all-start.3 = ((f32[16,8,256]{2,1,0:T(8,128)}), f32[16,8,256]{2,1,0:T(8,128)S(1)}, u32[]{:S(2)}, u32[]{:S(2)}) async-start(f32[16,8,256]{2,1,0:T(8,128)} %get-tuple-element.5), calls=%async_computation.3 | async-start | bytes 262144 | tf_op jit(solution)/shard_map/all_to_all | solution.py:232
  108.4 12.1 %all-to-all-start.4 = ((f32[16,8,256]{2,1,0:T(8,128)}), f32[16,8,256]{2,1,0:T(8,128)S(1)}, u32[]{:S(2)}, u32[]{:S(2)}) async-start(f32[16,8,256]{2,1,0:T(8,128)} %broadcast_in_dim.38), calls=%async_computation.4 | async-start | bytes 262144 | tf_op jit(solution)/shard_map/all_to_all | solution.py:232
  121.2 12.1 %all-to-all-start.5 = ((f32[16,8,256]{2,1,0:T(8,128)}), f32[16,8,256]{2,1,0:T(8,128)S(1)}, u32[]{:S(2)}, u32[]{:S(2)}) async-start(f32[16,8,256]{2,1,0:T(8,128)} %broadcast_in_dim.39), calls=%async_computation.5 | async-start | bytes 262144 | tf_op jit(solution)/shard_map/all_to_all | solution.py:232
  133.3 0.7 copy-start.1

commit v2 on v1

--- a/solution.py
+++ b/solution.py
@@ -9,6 +9,7 @@
 from jax.sharding import Mesh
 from jax.sharding import PartitionSpec as P
 
+
 f32 = jnp.float32
 bf16 = jnp.bfloat16
 
@@ -38,9 +39,10 @@
     return base
 
 
-def attention_kernel(x_ref, y_ref, out_ref, xa, ya, yw, sbuf, mbuf, acc, *, tile, sub):
+def attention_kernel(x_ref, own_ref, other_ref, out_ref, xa, ya, yw, sbuf, mbuf, acc, *, tile, sub):
     n_early, _, early_width = x_ref.shape
-    n_late, _, late_width = y_ref.shape
+    n_half, _, late_width = own_ref.shape
+    n_late = 2 * n_half
     pairs = n_early // 2
     tiles = n_late * late_width // tile
     wide = 2 * early_width
@@ -57,7 +59,7 @@
 
     lax.fori_loop(0, pairs, prepare_early, 0)
 
-    def prepare_late(b, carry):
+    def prepare_late(y_ref, b, slot):
         yb = y_ref[b, :DIM, :]
         y = yb.astype(f32)
         logs = y_ref[b, DIM : DIM + 8, :].astype(f32)[:1]
@@ -68,13 +70,17 @@
         t = jnp.concatenate([y, extra], 0).T
         lane = lax.broadcasted_iota(jnp.int32, (late_width, 128), 1)
         twice = jnp.where(lane < DIM, t, pltpu.roll(t, DIM, 1))
-        first = pl.multiple_of(b * late_width, late_width)
+        first = pl.multiple_of(slot * late_width, late_width)
         ya[pl.ds(first, late_width), :] = jnp.concatenate([t, twice], 1).astype(bf16)
         ones = jnp.where(lax.broadcasted_iota(jnp.int32, (16, late_width), 0) == 0, 1.0, 0.0)
         yw[:, pl.ds(first, late_width)] = jnp.concatenate([yb, ones.astype(bf16)], 0)
+
+    def prepare_both(b, carry):
+        prepare_late(own_ref, b, b)
+        prepare_late(other_ref, b, n_half + b)
         return carry
 
-    lax.fori_loop(0, n_late, prepare_late, 0)
+    lax.fori_loop(0, n_half, prepare_both, 0)
     acc[...] = jnp.zeros_like(acc)
     parts = tile // sub
 
@@ -120,15 +126,15 @@
     lax.fori_loop(0, steps // 2, two_steps, jnp.full((1, wide), LOWEST, f32))
 
 
-def attention(early_all, late_all, tile=2048, sub=512):
+def attention(early_all, late_own, late_other, tile=2048, sub=512):
     n_early, _, early_width = early_all.shape
-    n_late, _, late_width = late_all.shape
-    late_total = n_late * late_width
+    n_half, _, late_width = late_own.shape
+    late_total = 2 * n_half * late_width
     wide = 2 * early_width
     return pl.pallas_call(
         functools.partial(attention_kernel, tile=tile, sub=sub),
         out_shape=jax.ShapeDtypeStruct((n_early, 72, early_width), f32),
-        in_specs=[pl.BlockSpec(memory_space=pltpu.VMEM)] * 2,
+        in_specs=[pl.BlockSpec(memory_space=pltpu.VMEM)] * 3,
         out_specs=pl.BlockSpec(memory_space=pltpu.VMEM),
         scratch_shapes=[
             pltpu.VMEM((n_early // 2, 256, wide), bf16),
@@ -140,7 +146,7 @@
         ],
         compiler_params=pltpu.CompilerParams(vmem_limit_bytes=48 * 2**20),
         name="attention",
-    )(early_all, late_all)
+    )(early_all, late_own, late_other)
 
 
 def moments_kernel(got_ref, x_ref, label_ref, projected_ref, sums_ref):
@@ -182,50 +188,56 @@
         ),
         in_specs=[pl.BlockSpec(memory_space=pltpu.VMEM)] * 3,
         out_specs=(pl.BlockSpec(memory_space=pltpu.VMEM),) * 2,
+        compiler_params=pltpu.CompilerParams(vmem_limit_bytes=16 * 2**20),
         name="moments",
     )(got, early, labels)
 
 
-def correlate_kernel(sums_ref, split_ref, plain_ref, out_ref, right, *, cells):
-    @pl.when(pl.program_id(0) == 0)
-    def _():
-        by_class = sums_ref[:8].reshape(DIM, FATES) / cells
-        second = sums_ref[8:].reshape(DIM, FATES)[:, :128]
-        flipped = second.T
-        share = jnp.concatenate(
-            [flipped[DIM + q : DIM + q + 1] for q in range(FATES // DIM)], 1
-        ) / cells
-        mean = jnp.sum(by_class, 1, keepdims=True)
-        mean_row = jnp.broadcast_to(mean, (DIM, 128)).T[:1]
-        mean_row = jnp.concatenate([mean_row, jnp.zeros((1, 128 - DIM), f32)], 1)
-        lane = lax.broadcasted_iota(jnp.int32, (DIM, 128), 1)
-        square = jnp.where(lane < DIM, second, 0.0) / cells - mean * mean_row
-        cross = (by_class - mean * share) / jnp.sqrt(share * (1.0 - share))
-        both = jnp.concatenate([cross, square], 1)
-        high = both.astype(bf16)
-        low = (both - high.astype(f32)).astype(bf16)
-        right[...] = jnp.concatenate([high, high, low, low], 0)
-
-    product = jnp.dot(split_ref[...], right[...], preferred_element_type=f32)
-    variance = jnp.sum(product[:, FATES:] * plain_ref[...], 1, keepdims=True) + EPSILON
-    out_ref[...] = product[:, :FATES] * (1.0 / jnp.sqrt(variance))
-
-
-def correlate(sums, split, plain, cells, block=400):
+def correlate_kernel(sums_ref, split_ref, out_ref, right, stage, sems, *, cells, block):
+    genes = split_ref.shape[0]
+    by_class = sums_ref[:8].reshape(DIM, FATES) / cells
+    second = sums_ref[8:].reshape(DIM, FATES)[:, :128]
+    flipped = second.T
+    share = jnp.concatenate([flipped[DIM + q : DIM + q + 1] for q in range(FATES // DIM)], 1) / cells
+    mean = jnp.sum(by_class, 1, keepdims=True)
+    mean_row = jnp.broadcast_to(mean, (DIM, 128)).T[:1, :DIM]
+    square = second[:, :DIM] / cells - mean * mean_row
+    cross = (by_class - mean * share) / jnp.sqrt(share * (1.0 - share))
+    both = jnp.concatenate([cross, square, square], 1)
+    high = both.astype(bf16)
+    low = (both - high.astype(f32)).astype(bf16)
+    right[...] = jnp.concatenate([high, high, low, low], 0)
+
+    def copy(k):
+        rows = pl.ds(k * block, block)
+        return pltpu.make_async_copy(stage.at[rows], out_ref.at[rows], sems.at[k])
+
+    for k in range(genes // block):
+        rows = split_ref[k * block : (k + 1) * block]
+        product = jnp.dot(rows, right[...], preferred_element_type=f32)
+        halves = rows[:, :128].astype(f32)
+        variance = jnp.sum(product[:, FATES:] * halves, 1, keepdims=True) + EPSILON
+        stage[k * block : (k + 1) * block] = product[:, :FATES] * (1.0 / jnp.sqrt(variance))
+        copy(k).start()
+    for k in range(genes // block):
+        copy(k).wait()
+
+
+def correlate(sums, split, cells, block=400):
     genes = split.shape[0]
     return pl.pallas_call(
-        functools.partial(correlate_kernel, cells=cells),
-        grid=(genes // block,),
+        functools.partial(correlate_kernel, cells=cells, block=block),
         out_shape=jax.ShapeDtypeStruct((genes, FATES), f32),
-        in_specs=[
-            pl.BlockSpec((16, 8, FATES), lambda i: (0, 0, 0)),
-            pl.BlockSpec((block, 256), lambda i: (i, 0)),
-            pl.BlockSpec((block, 128), lambda i: (i, 0)),
+        in_specs=[pl.BlockSpec(memory_space=pltpu.VMEM)] * 2,
+        out_specs=pl.BlockSpec(memory_space=pl.ANY),
+        scratch_shapes=[
+            pltpu.VMEM((256, FATES + 128), bf16),
+            pltpu.VMEM((genes, FATES), f32),
+            pltpu.SemaphoreType.DMA((genes // block,)),
         ],
-        out_specs=pl.BlockSpec((block, FATES), lambda i: (i, 0)),
-        scratch_shapes=[pltpu.VMEM((256, FATES + 128), bf16)],
+        compiler_params=pltpu.CompilerParams(vmem_limit_bytes=16 * 2**20),
         name="correlate",
-    )(sums, split, plain)
+    )(sums, split)
 
 
 def exchange(blocks, axes):
@@ -236,24 +248,24 @@
     return exchange(jnp.broadcast_to(block[None], (16,) + block.shape), axes)
 
 
-def per_device(early, late, late_logs, labels, loadings):
+def program(early, late, late_logs, labels, loadings):
     cells = float(early.shape[1] * math.prod(SIZES))
     turned = loadings.T
     high = lax.reduce_precision(turned, 8, 7)
     low = turned - high
     split = jnp.concatenate([high, low, high, low], 1).astype(bf16)
-    plain = jnp.pad(turned, ((0, 0), (0, 128 - DIM)))
 
     late_full = jnp.concatenate([late, late_logs[None], jnp.zeros((7,) + late_logs.shape, bf16)], 0)
     early_all = spread(early, EARLY_GROUP)
-    late_all = spread(late_full, LATE_GROUP)
-    partial = attention(early_all, late_all)
+    late_own = lax.all_gather(late_full, "z", axis=0, tiled=False)
+    late_other = lax.ppermute(late_own, "core", [(0, 1), (1, 0)])
+    partial = attention(early_all, late_own, late_other)
     got = exchange(partial, EARLY_GROUP)
     projected, sums = moments(got, early, labels[None])
     sums = jnp.sum(exchange(sums, EARLY_GROUP), 0)
     sums = jnp.sum(spread(sums, LATE_GROUP), 0)
     sums = spread(sums, EARLY_GROUP)
-    return projected, correlate(sums, split, plain, cells)
+    return projected, correlate(sums, split, cells)
 
 
 def solution(mesh):
@@ -261,5 +273,5 @@
     in_specs = (P(None, AXES), P(None, AXES), P(AXES), P(AXES), P())
     out_specs = (P(None, AXES), P())
     return jax.shard_map(
-        per_device, mesh=named, in_specs=in_specs, out_specs=out_specs, check_vma=False
+        program, mesh=named, in_specs=in_specs, out_specs=out_specs, check_vma=False
     )

time: 142 us -> 125 us (0.88)
  starting transfers between devices: 20.5 us -> 14.3 us
  Pallas kernels: 28.6 us -> 22.8 us
  waiting for transfers between devices: 25 us -> 21.2 us
  blocking collectives: 56.2 us -> 58.9 us
  local copies, waits for them, and re-layouts: 5.7 us -> 3.26 us
    all_gather x0 -> x1, blocking collectives: none -> 29.3 us  [program(): late_own = lax.all_gather(late_full, 'z', axis=0, tiled=False)]
    all_to_all x2, blocking collectives: 56.2 us -> 29.7 us  [exchange(): return lax.all_to_all(blocks, axes, 0, 0, tiled=False)]
    all_to_all x4 -> x3, starting transfers between devices: 20.5 us -> 14.3 us  [exchange(): return lax.all_to_all(blocks, axes, 0, 0, tiled=False)]
    all_to_all x4 -> x3, waiting for transfers between devices: 25 us -> 21.2 us  [exchange(): return lax.all_to_all(blocks, axes, 0, 0, tiled=False)]
    pallas_call x1, Pallas kernels: 5.55 us -> 1.94 us  [correlate(): pl.pallas_call(functools.partial(correlate_kernel, cells=cells, block=blo...]
    broadcast_in_dim x4 -> x3, local copies, waits for them, and re-layouts: 2.88 us -> 2.15 us  [spread(): return exchange(jnp.broadcast_to(block[None], (16,) + block.shape), axes)]
  transfers between devices with their start and end apart: 4 -> 4, of which waited for: 4 -> 3; matrix products, arithmetic and copies ran while one was open for 4% -> 2% of each run, Pallas kernels for 0% -> 0%
where the time goes in v2:
time: 125 us; the launch traced here: 123 us
  blocking collectives  58.9 us (47%)
  Pallas kernels  22.8 us (18%)
  waiting for transfers between devices  21.2 us (17%)
  starting transfers between devices  14.3 us (11%)
  local copies, waits for them, and re-layouts  3.26 us (3%)
  other arithmetic  1.82 us (1%)
    all_to_all x2, blocking collectives, exchange(): return lax.all_to_all(blocks, axes, 0, 0, tiled=False)  29.7 us
    all_gather x1, blocking collectives, program(): late_own = lax.all_gather(late_full, 'z', axis=0, tiled=False)  29.3 us
    all_to_all x3, waiting for transfers between devices, exchange(): return lax.all_to_all(blocks, axes, 0, 0, tiled=False)  21.2 us
    pallas_call x1, Pallas kernels, attention(): pl.pallas_call(functools.partial(attention_kernel, tile=tile, sub=sub), o...  19.9 us
    all_to_all x3, starting transfers between devices, exchange(): return lax.all_to_all(blocks, axes, 0, 0, tiled=False)  14.3 us
  transfers between devices with their start and end apart: 4, of which 3 were waited for; matrix products, arithmetic and copies ran while one was open for 2% of the time, Pallas kernels for 0%

profile of v2, /device:TPU:2, one launch (start us, length us, event | category | flops | bytes accessed | tf_op | source)
XLA Modules:
  0.0 123.1 jit_solution(14547227137971349022)
XLA Ops:
  0.6 0.7 broadcast_in_dim.13
  1.3 0.1 pad.6.clone
  1.4 0.9 maximum_maximum_fusion
  2.3 29.3 %all-gather = bf16[576,512]{1,0:T(8,128)(2,1)S(1)} all-gather(bf16[72,512]{1,0:T(8,128)(2,1)S(1)} %maximum_maximum_fusion), channel_id=2, replica_groups=mesh['yl'=2,'z'=8,'yh'=2,'x'=4,'core'=2] {'z'}, dimensions={0}, use_global_device_ids=true | all-gather | bytes 663552 | tf_op jit(solution)/shard_map/all_gather | solution.py:260
  31.6 0.0 collective-permute-start
  31.6 0.8 broadcast_in_dim.12
  32.4 15.2 %all_to_all.25.x_ref = bf16[16,64,128]{2,1,0:T(8,128)(2,1)S(1)} all-to-all(bf16[16,64,128]{2,1,0:T(8,128)(2,1)S(1)} %broadcast_in_dim.12), channel_id=1, replica_groups=mesh['yl'=2,'z'=8,'yh'=2,'x'=4,'core'=2] {'yl','yh','x'}, dimensions={0} | all-to-all | bytes 524288 | tf_op jit(solution)/shard_map/all_to_all | solution.py:244
  47.6 0.0 collective-permute-done.other_ref
  47.6 19.9 %attention.1 = f32[16,72,128]{2,1,0:T(8,128)S(1)} custom-call(bf16[16,64,128]{2,1,0:T(8,128)(2,1)S(1)} %all_to_all.25.x_ref, bf16[8,72,512]{2,1,0:T(8,128)(2,1)S(1)} %bitcast.6, bf16[8,72,512]{2,1,0:T(8,128)(2,1)S(1)} %collective-permute-done.other_ref), custom_call_target="tpu_custom_call" | custom-call | tf_op jit(solution)/shard_map/attention/pallas_call | solution.py:134
  67.5 14.5 %all_to_all.26.got_ref = f32[16,72,128]{2,1,0:T(8,128)S(1)} all-to-all(f32[16,72,128]{2,1,0:T(8,128)S(1)} %attention.1), channel_id=1, replica_groups=mesh['yl'=2,'z'=8,'yh'=2,'x'=4,'core'=2] {'yl','yh','x'}, dimensions={0} | all-to-all | bytes 1179648 | tf_op jit(solution)/shard_map/all_to_all | solution.py:244
  82.0 0.0 copy-done
  82.0 1.0 moments.1
  83.0 4.7 %all-to-all-start.2 = ((f32[16,8,256]{2,1,0:T(8,128)}), f32[16,8,256]{2,1,0:T(8,128)S(1)}, u32[]{:S(2)}, u32[]{:S(2)}) async-start(f32[16,8,256]{2,1,0:T(8,128)} %get-tuple-element.5), calls=%async_computation.2 | async-start | bytes 262144 | tf_op jit(solution)/shard_map/all_to_all | solution.py:244
  87.7 0.3 copy.8
  88.0 6.4 %all-to-all-done.2 = f32[16,8,256]{2,1,0:T(8,128)S(1)} async-done(((f32[16,8,256]{2,1,0:T(8,128)}), f32[16,8,256]{2,1,0:T(8,128)S(1)}, u32[]{:S(2)}, u32[]{:S(2)}) %all-to-all-start.2) | async-done | bytes 131104 | tf_op jit(solution)/shard_map/all_to_all | solution.py:244
  94.4 0.7 broadcast_in_dim.31
  95.1 4.8 %all-to-all-start.3 = ((f32[16,8,256]{2,1,0:T(8,128)}), f32[16,8,256]{2,1,0:T(8,128)S(1)}, u32[]{:S(2)}, u32[]{:S(2)}) async-start(f32[16,8,256]{2,1,0:T(8,128)} %broadcast_in_dim.31), calls=%async_computation.3 | async-start | bytes 262144 | tf_op jit(solution)/shard_map/all_to_all | solution.py:244
  100.0 0.2 reduce-precision_convert_fusion
  100.1 8.5 %all-to-all-done.3 = f32[16,8,256]{2,1,0:T(8,128)S(1)} async-done(((f32[16,8,256]{2,1,0:T(8,128)}), f32[16,8,256]{2,1,0:T(8,128)S(1)}, u32[]{:S(2)}, u32[]{:S(2)}) %all-to-all-start.3) | async-done | bytes 131104 | tf_op jit(solution)/shard_map/all_to_all | solution.py:244
  108.6 0.7 broadcast_in_dim.32
  109.3 4.8 %all-to-all-start.4 = ((f32[16,8,256]{2,1,0:T(8,128)}), f32[16,8,256]{2,1,0:T(8,128)S(1)}, u32[]{:S(2)}, u32[]{:S(2)}) async-start(f32[16,8,256]{2,1,0:T(8,128)} %broadcast_in_dim.32), calls=%async_computation.4 | async-start | bytes 262144 | tf_op jit(solution)/shard_map/all_to_all | solution.py:244
  114.1 0.7 pad_maximum_fusion.split_ref
  114.8 6.4 %all-to-all-done.4.sums_ref = f32[16,8,256]{2,1,0:T(8,128)S(1)} async-done(((f32[16,8,256]{2,1,0:T(8,128)}), f32[16,8,256]{2,1,0:T(8,128)S(1)}, u32[]{:S(2)}, u32[]{:S(2)}) %all-to-all-start.4) | async-done | bytes 131104 | tf_op jit(solution)/shard_map/all_to_all | solution.py:244
  121.2 1.9 %correlate.1 = f32[2000,256]{1,0:T(8,128)} custom-call(f32[16,8,256]{2,1,0:T(8,128)S(1)} %all-to-all-done.4.sums_ref, bf16[2000,256]{1,0:T(8,128)(2,1)S(1)} %pad_maximum_fusion.split_ref), custom_call_target="tpu_custom_call" | custom-call | tf_op jit(solution)/shard_map/correlate/pallas_call | solution.py:228
  (8 shorter events, 0.1 us)
Async XLA Ops:
  31.6 50.4 %copy-start = (bf16[64,128]{1,0:T(8,128)(2,1)S(1)}, bf16[64,128]{1,0:T(8,128)(2,1)}, u32[]{:S(2)}) copy-start(bf16[64,128]{1,0:T(8,128)(2,1)} %x_ref.1) | copy-start | bytes 49156
  31.6 50.4 %copy-start.1 = (s32[128]{0:T(128)S(1)}, s32[128]{0:T(128)}, u32[]{:S(2)}) copy-start(s32[128]{0:T(128)} %param.8) | copy-start | bytes 1540
  31.6 16.0 %collective-permute-start = (bf16[8,72,512]{2,1,0:T(8,128)(2,1)S(1)}, bf16[8,72,512]{2,1,0:T(8,128)(2,1)S(1)}, u32[]{:S(2)}, u32[]{:S(2)}) collective-permute-start(bf16[8,72,512]{2,1,0:T(8,128)(2,1)S(1)} %bitcast.5), channel_id=1, source_target_pairs={{0,1},{1,0},{2,3},{3,2},{4,5},{5,4},{6,7},{7,6},{8,9},{9,8},{10,11... | collective-permute-start | bytes 1769480 | tf_op jit(solution)/shard_map/ppermute | solution.py:261
  47.6 40.1 %copy-start.2 = (f32[64,2000]{1,0:T(8,128)S(1)}, f32[64,2000]{1,0:T(8,128)}, u32[]{:S(2)}) copy-start(f32[64,2000]{1,0:T(8,128)} %param.9) | copy-start | bytes 1536004
  83.0 11.4 %all-to-all-start.2 = ((f32[16,8,256]{2,1,0:T(8,128)}), f32[16,8,256]{2,1,0:T(8,128)S(1)}, u32[]{:S(2)}, u32[]{:S(2)}) async-start(f32[16,8,256]{2,1,0:T(8,128)} %get-tuple-element.5), calls=%async_computation.2 | async-start | bytes 262144 | tf_op jit(solution)/shard_map/all_to_all | solution.py:244
  95.1 13.5 %all-to-all-start.3 = ((f32[16,8,256]{2,1,0:T(8,128)}), f32[16,8,256]{2,1,0:T(8,128)S(1)}, u32[]{:S(2)}, u32[]{:S(2)}) async-start(f32[16,8,256]{2,1,0:T(8,128)} %broadcast_in_dim.31), calls=%async_computation.3 | async-start | bytes 262144 | tf_op jit(solution)/shard_map/all_to_all | solution.py:244
  109.3 11.9 %all-to-all-start.4 = ((f32[16,8,256]{2,1,0:T(8,128)}), f32[16,8,256]{2,1,0:T(8,128)S(1)}, u32[]{:S(2)}, u32[]{:S(2)}) async-start(f32[16,8,256]{2,1,0:T(8,128)} %broadcast_in_dim.32), calls=%async_computation.4 | async-start | bytes 262144 | tf_op jit(solution)/shard_map/all_to_all | solution.py:244

commit v3 on v2

--- a/solution.py
+++ b/solution.py
@@ -39,61 +39,105 @@
     return base
 
 
-def attention_kernel(x_ref, own_ref, other_ref, out_ref, xa, ya, yw, sbuf, mbuf, acc, *, tile, sub):
-    n_early, _, early_width = x_ref.shape
-    n_half, _, late_width = own_ref.shape
-    n_late = 2 * n_half
-    pairs = n_early // 2
-    tiles = n_late * late_width // tile
-    wide = 2 * early_width
-
-    def prepare_early(b, carry):
-        x = jnp.concatenate([x_ref[2 * b], x_ref[2 * b + 1]], 1).astype(f32)
-        norms = jnp.sum(x * x, 0, keepdims=True)
-        high, mid, low = split3(x * (2.0 * SHARP * LOG2E))
+def pack_kernel(late_ref, log_ref, one_ref, all_ref):
+    cells = late_ref.shape[1]
+    blocks = [late_ref[:, 128 * k : 128 * (k + 1)] for k in range(cells // 128)]
+    logs = [log_ref[:, 128 * k : 128 * (k + 1)].astype(f32) for k in range(cells // 128)]
+    tail = jnp.concatenate(logs + [jnp.zeros((8 - cells // 128, 128), f32)], 0).astype(bf16)
+    one = jnp.concatenate(blocks + [tail], 0)
+    one_ref[0] = one
+    for k in range(all_ref.shape[0]):
+        all_ref[k] = one
+
+
+def pack(late, logs, copies):
+    rows = DIM * late.shape[1] // 128 + 8
+    return pl.pallas_call(
+        pack_kernel,
+        out_shape=(
+            jax.ShapeDtypeStruct((1, rows, 128), bf16),
+            jax.ShapeDtypeStruct((copies, rows, 128), bf16),
+        ),
+        in_specs=[pl.BlockSpec(memory_space=pltpu.VMEM)] * 2,
+        out_specs=(pl.BlockSpec(memory_space=pltpu.VMEM),) * 2,
+        compiler_params=pltpu.CompilerParams(vmem_limit_bytes=8 * 2**20),
+        name="pack",
+    )(late, logs[None])
+
+
+def attention_kernel(*refs, n_x, n_late, skip, tile, parts, has_state):
+    refs = list(refs)
+    slot_ref = refs.pop(0)
+    x_refs = [refs.pop(0) for _ in range(n_x)]
+    late_refs = [refs.pop(0) for _ in range(n_late)]
+    if has_state:
+        xa, state_ref = x_refs[0], refs.pop(0)
+        out_ref = refs.pop(0)
+    else:
+        out_ref, xa = refs.pop(0), refs.pop(0)
+    ya, yw, sbuf, mbuf, acc = refs
+    wide = 256
+    pairs = xa.shape[0]
+    chunk = (late_refs[0].shape[1] - 8) * 2
+    groups = chunk // 128
+    chunks = sum(r.shape[0] - skip for r in late_refs)
+    tiles = chunks * chunk // tile
+
+    if not has_state:
         row = lax.broadcasted_iota(jnp.int32, (DIM, wide), 0)
-        extra = jnp.where(row < 3, 1.0, jnp.zeros((DIM, wide), f32))
-        extra = put_rows(extra, row, 3, norms * (-SHARP * LOG2E))
-        xa[b] = jnp.concatenate([high, extra, mid, low], 0).astype(bf16)
-        return carry
-
-    lax.fori_loop(0, pairs, prepare_early, 0)
+        blank = jnp.where(row < 3, 1.0, jnp.zeros((DIM, wide), f32))
+        per = x_refs[0].shape[0] // 2
+        for b in range(pairs):
+            ref, k = x_refs[b // per], 2 * (b % per)
+            x = jnp.concatenate([ref[k], ref[k + 1]], 1).astype(f32)
+            norms = jnp.sum(x * x, 0, keepdims=True)
+            high, mid, low = split3(x * (2.0 * SHARP * LOG2E))
+            extra = put_rows(blank, row, 3, norms * (-SHARP * LOG2E))
+            xa[b] = jnp.concatenate([high, extra, mid, low], 0).astype(bf16)
 
     def prepare_late(y_ref, b, slot):
-        yb = y_ref[b, :DIM, :]
+        yb = jnp.concatenate([y_ref[b, DIM * k : DIM * (k + 1), :] for k in range(groups)], 1)
+        tail = y_ref[b, DIM * groups : DIM * groups + 8, :].astype(f32)
+        logs = jnp.concatenate([tail[k : k + 1] for k in range(groups)], 1)
         y = yb.astype(f32)
-        logs = y_ref[b, DIM : DIM + 8, :].astype(f32)[:1]
         bias = (logs - jnp.sum(y * y, 0, keepdims=True) * SHARP) * LOG2E
-        row = lax.broadcasted_iota(jnp.int32, (DIM, late_width), 0)
-        extra = jnp.where((row >= 3) & (row < 6), 1.0, jnp.zeros((DIM, late_width), f32))
+        row = lax.broadcasted_iota(jnp.int32, (DIM, chunk), 0)
+        extra = jnp.where((row >= 3) & (row < 6), 1.0, jnp.zeros((DIM, chunk), f32))
         extra = put_rows(extra, row, 0, bias)
         t = jnp.concatenate([y, extra], 0).T
-        lane = lax.broadcasted_iota(jnp.int32, (late_width, 128), 1)
+        lane = lax.broadcasted_iota(jnp.int32, (chunk, 128), 1)
         twice = jnp.where(lane < DIM, t, pltpu.roll(t, DIM, 1))
-        first = pl.multiple_of(slot * late_width, late_width)
-        ya[pl.ds(first, late_width), :] = jnp.concatenate([t, twice], 1).astype(bf16)
-        ones = jnp.where(lax.broadcasted_iota(jnp.int32, (16, late_width), 0) == 0, 1.0, 0.0)
-        yw[:, pl.ds(first, late_width)] = jnp.concatenate([yb, ones.astype(bf16)], 0)
-
-    def prepare_both(b, carry):
-        prepare_late(own_ref, b, b)
-        prepare_late(other_ref, b, n_half + b)
-        return carry
-
-    lax.fori_loop(0, n_half, prepare_both, 0)
+        first = pl.multiple_of(slot * chunk, chunk)
+        ya[pl.ds(first, chunk), :] = jnp.concatenate([t, twice], 1).astype(bf16)
+        ones = jnp.where(lax.broadcasted_iota(jnp.int32, (16, chunk), 0) == 0, 1.0, 0.0)
+        yw[:, pl.ds(first, chunk)] = jnp.concatenate([yb, ones.astype(bf16)], 0)
+
+    if skip:
+        here = slot_ref[2 * pairs]
+        count = late_refs[0].shape[0]
+
+        def prepare(j, carry):
+            for k, ref in enumerate(late_refs):
+                prepare_late(ref, (here + 1 + j) % count, k * (count - 1) + j)
+            return carry
+
+        lax.fori_loop(0, count - 1, prepare, 0)
+    else:
+        for k, ref in enumerate(late_refs):
+            prepare_late(ref, 0, k)
     acc[...] = jnp.zeros_like(acc)
-    parts = tile // sub
-
-    def score_part(pair, first, j, slot, top):
-        s = jnp.dot(ya[pl.ds(first + j * sub, sub), :], xa[pair], preferred_element_type=f32)
-        sbuf[slot, j * sub : (j + 1) * sub, :] = s
-        here = jnp.max(s.reshape(sub // 8, 8, wide), 0)
+
+    def score_part(pair, first, offset, size, slot, top):
+        s = jnp.dot(ya[pl.ds(first + offset, size), :], xa[pair], preferred_element_type=f32)
+        sbuf[slot, offset : offset + size, :] = s
+        here = jnp.max(s.reshape(size // 8, 8, wide), 0)
         return here if top is None else jnp.maximum(top, here)
 
     steps = pairs * tiles
+    spans = [(sum(parts[:k]), parts[k]) for k in range(len(parts))]
     top = None
-    for j in range(parts):
-        top = score_part(0, 0, j, 0, top)
+    for offset, size in spans:
+        top = score_part(0, 0, offset, size, 0, top)
     mbuf[0] = top
 
     def step(n, slot, before):
@@ -101,23 +145,31 @@
         first = pl.multiple_of((n % tiles) * tile, tile)
         following = jnp.minimum(n + 1, steps - 1)
         next_first = pl.multiple_of((following % tiles) * tile, tile)
-        before = jnp.where(n % tiles == 0, LOWEST, before)
+        fresh = n % tiles == 0
+        left, right = slot_ref[2 * pair], slot_ref[2 * pair + 1]
+        carried = acc[...]
+        if has_state:
+            state = jnp.concatenate([state_ref[left], state_ref[right]], 1)
+            before = jnp.where(fresh, state[DIM + 1 : DIM + 2], before)
+            carried = jnp.where(fresh, state, carried)
+        else:
+            before = jnp.where(fresh, LOWEST, before)
         now = jnp.maximum(before, jnp.max(mbuf[slot], 0, keepdims=True))
         shrink = jnp.exp2(before - now)
         top = None
         sums = None
-        for j in range(parts):
-            top = score_part(following // tiles, next_first, j, 1 - slot, top)
-            weights = jnp.exp2(sbuf[slot, j * sub : (j + 1) * sub, :] - now).astype(bf16)
-            more = jnp.dot(yw[:, pl.ds(first + j * sub, sub)], weights, preferred_element_type=f32)
+        for offset, size in spans:
+            top = score_part(following // tiles, next_first, offset, size, 1 - slot, top)
+            weights = jnp.exp2(sbuf[slot, offset : offset + size, :] - now).astype(bf16)
+            more = jnp.dot(yw[:, pl.ds(first + offset, size)], weights, preferred_element_type=f32)
             sums = more if sums is None else sums + more
         mbuf[1 - slot] = top
-        total = acc[...] * shrink + sums
-        acc[...] = total
+        total = carried * shrink + sums[:72]
         row = lax.broadcasted_iota(jnp.int32, (72, wide), 0)
-        packed = jnp.where(row == DIM + 1, now, total[:72])
-        out_ref[2 * pair] = packed[:, :early_width]
-        out_ref[2 * pair + 1] = packed[:, early_width:]
+        packed = jnp.where(row == DIM + 1, now, total)
+        acc[...] = packed
+        out_ref[left] = packed[:, :128]
+        out_ref[right] = packed[:, 128:]
         return now
 
     def two_steps(i, before):
@@ -126,27 +178,39 @@
     lax.fori_loop(0, steps // 2, two_steps, jnp.full((1, wide), LOWEST, f32))
 
 
-def attention(early_all, late_own, late_other, tile=2048, sub=512):
-    n_early, _, early_width = early_all.shape
-    n_half, _, late_width = late_own.shape
-    late_total = 2 * n_half * late_width
-    wide = 2 * early_width
+def attention(slots, early, late, state=None, skip=0, tile=1024, parts=(512, 512)):
+    wide = 256
+    pairs = early[0].shape[0] if state is not None else sum(e.shape[0] for e in early) // 2
+    late_total = sum(r.shape[0] - skip for r in late) * (late[0].shape[1] - 8) * 2
+    out_shape = [jax.ShapeDtypeStruct((2 * pairs, 72, 128), f32)]
+    operands = list(early) + list(late)
+    if state is None:
+        out_shape.append(jax.ShapeDtypeStruct((pairs, 256, wide), bf16))
+    else:
+        operands.append(state)
+    vmem = pl.BlockSpec(memory_space=pltpu.VMEM)
     return pl.pallas_call(
-        functools.partial(attention_kernel, tile=tile, sub=sub),
-        out_shape=jax.ShapeDtypeStruct((n_early, 72, early_width), f32),
-        in_specs=[pl.BlockSpec(memory_space=pltpu.VMEM)] * 3,
-        out_specs=pl.BlockSpec(memory_space=pltpu.VMEM),
+        functools.partial(
+            attention_kernel,
+            n_x=len(early),
+            n_late=len(late),
+            skip=skip,
+            tile=tile,
+            parts=parts,
+            has_state=state is not None,
+        ),
+        out_shape=out_shape,
+        in_specs=[pl.BlockSpec(memory_space=pltpu.SMEM)] + [vmem] * len(operands),
+        out_specs=[vmem] * len(out_shape),
         scratch_shapes=[
-            pltpu.VMEM((n_early // 2, 256, wide), bf16),
             pltpu.VMEM((late_total, 256), bf16),
             pltpu.VMEM((80, late_total), bf16),
             pltpu.VMEM((2, tile, wide), f32),
             pltpu.VMEM((2, 8, wide), f32),
-            pltpu.VMEM((80, wide), f32),
+            pltpu.VMEM((72, wide), f32),
         ],
-        compiler_params=pltpu.CompilerParams(vmem_limit_bytes=48 * 2**20),
-        name="attention",
-    )(early_all, late_own, late_other)
+        compiler_params=pltpu.CompilerParams(vmem_limit_bytes=32 * 2**20),
+    )(slots, *operands)
 
 
 def moments_kernel(got_ref, x_ref, label_ref, projected_ref, sums_ref):
@@ -240,6 +304,15 @@
     )(sums, split)
 
 
+def shift(n, k):
+    return [(i, (i + k) % n) for i in range(n)]
+
+
+def shift_y(k):
+    place = [y % 2 * 2 + y // 2 for y in range(4)]
+    return [(place[y], place[(y + k) % 4]) for y in range(4)]
+
+
 def exchange(blocks, axes):
     return lax.all_to_all(blocks, axes, 0, 0, tiled=False)
 
@@ -255,11 +328,23 @@
     low = turned - high
     split = jnp.concatenate([high, low, high, low], 1).astype(bf16)
 
-    late_full = jnp.concatenate([late, late_logs[None], jnp.zeros((7,) + late_logs.shape, bf16)], 0)
-    early_all = spread(early, EARLY_GROUP)
-    late_own = lax.all_gather(late_full, "z", axis=0, tiled=False)
-    late_other = lax.ppermute(late_own, "core", [(0, 1), (1, 0)])
-    partial = attention(early_all, late_own, late_other)
+    late_one, late_copies = pack(late, late_logs, SIZES[1])
+    late_own = exchange(late_copies, "z")
+    swap = [(0, 1), (1, 0)]
+    late_near = lax.ppermute(late_one, "core", swap)
+    line = [early] + [lax.ppermute(early, "x", shift(4, k)) for k in range(1, 4)]
+    line = jnp.stack(line)
+    early_all = [line] + [lax.ppermute(line, ("yl", "yh"), shift_y(k)) for k in range(1, 4)]
+    y, x = 2 * lax.axis_index("yh") + lax.axis_index("yl"), lax.axis_index("x")
+    back = jnp.arange(16, dtype=jnp.int32)
+    to_y, to_x = (y - back // 4) % 4, (x - back % 4) % 4
+    slots = to_y % 2 * 8 + to_y // 2 * 4 + to_x
+    slots = jnp.concatenate([slots, lax.axis_index("z")[None]]).astype(jnp.int32)
+    partial, prepared = attention(slots, early_all, [late_one, late_near])
+    late_other = lax.ppermute(late_own, "core", swap)
+    rest = dict(skip=1, tile=1792, parts=(512, 512, 512, 256))
+    (partial,) = attention(slots, [prepared], [late_own], partial, **rest)
+    (partial,) = attention(slots, [prepared], [late_other], partial, **rest)
     got = exchange(partial, EARLY_GROUP)
     projected, sums = moments(got, early, labels[None])
     sums = jnp.sum(exchange(sums, EARLY_GROUP), 0)

time: 125 us -> 128 us (1.024)
  blocking collectives: 58.9 us -> 42.7 us
  starting transfers between devices: 14.3 us -> 23.7 us
  waiting for transfers between devices: 21.2 us -> 26.4 us
  Pallas kernels: 22.8 us -> 27.5 us
    all_gather x1 -> x0, blocking collectives: 29.3 us -> none  [program(): late_own = lax.all_gather(late_full, 'z', axis=0, tiled=False)]
    all_to_all x2, blocking collectives: 29.7 us -> 42.7 us  [exchange(): return lax.all_to_all(blocks, axes, 0, 0, tiled=False)]
    ppermute x1 -> x8, starting transfers between devices: 0.01 us -> 10.7 us  [the longest x3 5.9 us: program(): lax.ppermute(line, ('yl', 'yh'), shift_y(k))]
    ppermute x1 -> x8, waiting for transfers between devices: 0.01 us -> 4.99 us  [the longest x3 2.84 us: program(): lax.ppermute(line, ('yl', 'yh'), shift_y(k))]
    pallas_call x1 -> x4, Pallas kernels: 19.9 us -> 24.6 us  [the longest x3 24.5 us: attention(): pl.pallas_call(functools.partial(attention_kernel, n_x=len(early), n_late...]
  transfers between devices with their start and end apart: 4 -> 11, of which waited for: 3 -> 7; matrix products, arithmetic and copies ran while one was open for 2% -> 2% of each run, Pallas kernels for 0% -> 11%
where the time goes in v3:
time: 128 us; the launch traced here: 126 us
  blocking collectives  42.7 us (33%)
  Pallas kernels  27.5 us (21%)
  waiting for transfers between devices  26.4 us (21%)
  starting transfers between devices  23.7 us (19%)
  local copies, waits for them, and re-layouts  3.2 us (2%)
  other arithmetic  1.73 us (1%)
    all_to_all x2, blocking collectives, exchange(): return lax.all_to_all(blocks, axes, 0, 0, tiled=False)  42.7 us
    pallas_call x3, Pallas kernels, attention(): pl.pallas_call(functools.partial(attention_kernel, n_x=len(early), n_late...  24.5 us
    all_to_all x3, waiting for transfers between devices, exchange(): return lax.all_to_all(blocks, axes, 0, 0, tiled=False)  21.4 us
    all_to_all x3, starting transfers between devices, exchange(): return lax.all_to_all(blocks, axes, 0, 0, tiled=False)  13.1 us
    ppermute x3, starting transfers between devices, program(): lax.ppermute(line, ('yl', 'yh'), shift_y(k))  5.9 us
    ppermute x3, starting transfers between devices, program(): lax.ppermute(early, 'x', shift(4, k))  4.76 us
    ppermute x3, waiting for transfers between devices, program(): lax.ppermute(line, ('yl', 'yh'), shift_y(k))  2.84 us
  transfers between devices with their start and end apart: 11, of which 7 were waited for; matrix products, arithmetic and copies ran while one was open for 2% of the time, Pallas kernels for 11%

profile of v3, /device:TPU:2, one launch (start us, length us, event | category | flops | bytes accessed | tf_op | source)
XLA Modules:
  0.0 126.1 jit_solution(12088278854968421000)
XLA Ops:
  1.3 0.8 copy-done
  2.2 26.1 %all_to_all.25.refs_2_ = bf16[8,264,128]{2,1,0:T(8,128)(2,1)S(1)} all-to-all(bf16[8,264,128]{2,1,0:T(8,128)(2,1)S(1)} %get-tuple-element.10), channel_id=1, replica_groups=mesh['yl'=2,'z'=8,'yh'=2,'x'=4,'core'=2] {'z'}, dimensions={0} | all-to-all | bytes 1081344 | tf_op jit(solution)/shard_map/all_to_all | solution.py:317
  28.3 1.5 %collective-permute-start = (bf16[64,128]{1,0:T(8,128)(2,1)}, bf16[64,128]{1,0:T(8,128)(2,1)S(1)}, u32[]{:S(2)}, u32[]{:S(2)}) collective-permute-start(bf16[64,128]{1,0:T(8,128)(2,1)} %x_ref.1), channel_id=1, source_target_pairs={{0,2},{2,4},{4,6},{6,0},{1,3},{3,5},{5,7},{7,1},{8,10},{10,12},{12... | collective-permute-start | bytes 49160 | tf_op jit(solution)/shard_map/ppermute | solution.py:335
  29.8 1.1 collective-permute-start.1
  31.0 2.2 %collective-permute-start.2 = (bf16[64,128]{1,0:T(8,128)(2,1)}, bf16[64,128]{1,0:T(8,128)(2,1)S(1)}, u32[]{:S(2)}, u32[]{:S(2)}) collective-permute-start(bf16[64,128]{1,0:T(8,128)(2,1)} %x_ref.1), channel_id=1, source_target_pairs={{0,6},{2,0},{4,2},{6,4},{1,7},{3,1},{5,3},{7,5},{8,14},{10,8},{12,... | collective-permute-start | bytes 49160 | tf_op jit(solution)/shard_map/ppermute | solution.py:335
  33.1 2.1 %collective-permute-done.1 = bf16[64,128]{1,0:T(8,128)(2,1)S(1)} collective-permute-done((bf16[64,128]{1,0:T(8,128)(2,1)}, bf16[64,128]{1,0:T(8,128)(2,1)S(1)}, u32[]{:S(2)}, u32[]{:S(2)}) %collective-permute-start.1) | collective-permute-done | bytes 16416 | tf_op jit(solution)/shard_map/ppermute | solution.py:335
  35.3 0.7 pad_maximum_fusion.1.refs_1_
  36.0 1.7 %collective-permute-start.3 = (bf16[4,64,128]{2,1,0:T(8,128)(2,1)S(1)}, bf16[4,64,128]{2,1,0:T(8,128)(2,1)S(1)}, u32[]{:S(2)}, u32[]{:S(2)}) collective-permute-start(bf16[4,64,128]{2,1,0:T(8,128)(2,1)S(1)} %pad_maximum_fusion.1.refs_1_), channel_id=1, source_target_pairs={{0,128},{128,8},{8,136},{136,0},{1,129},{129,9},{9,137},{137,1},{2... | collective-permute-start | bytes 196616 | tf_op jit(solution)/shard_map/ppermute | solution.py:337
  37.7 2.9 %collective-permute-start.4 = (bf16[4,64,128]{2,1,0:T(8,128)(2,1)S(1)}, bf16[4,64,128]{2,1,0:T(8,128)(2,1)S(1)}, u32[]{:S(2)}, u32[]{:S(2)}) collective-permute-start(bf16[4,64,128]{2,1,0:T(8,128)(2,1)S(1)} %pad_maximum_fusion.1.refs_1_), channel_id=1, source_target_pairs={{0,8},{128,136},{8,0},{136,128},{1,9},{129,137},{9,1},{137,129},{2... | collective-permute-start | bytes 196616 | tf_op jit(solution)/shard_map/ppermute | solution.py:337
  40.6 1.3 %collective-permute-start.5 = (bf16[4,64,128]{2,1,0:T(8,128)(2,1)S(1)}, bf16[4,64,128]{2,1,0:T(8,128)(2,1)S(1)}, u32[]{:S(2)}, u32[]{:S(2)}) collective-permute-start(bf16[4,64,128]{2,1,0:T(8,128)(2,1)S(1)} %pad_maximum_fusion.1.refs_1_), channel_id=1, source_target_pairs={{0,136},{128,0},{8,128},{136,8},{1,137},{129,1},{9,129},{137,9},{2... | collective-permute-start | bytes 196616 | tf_op jit(solution)/shard_map/ppermute | solution.py:337
  42.3 1.2 collective-permute-done.4.refs_3_
  43.5 1.3 %collective-permute-done.5.refs_4_ = bf16[4,64,128]{2,1,0:T(8,128)(2,1)S(1)} collective-permute-done((bf16[4,64,128]{2,1,0:T(8,128)(2,1)S(1)}, bf16[4,64,128]{2,1,0:T(8,128)(2,1)S(1)}, u32[]{:S(2)}, u32[]{:S(2)}) %collective-permute-start.5) | collective-permute-done | bytes 65568 | tf_op jit(solution)/shard_map/ppermute | solution.py:337
  44.9 3.9 %shard_map.68 = (f32[16,72,128]{2,1,0:T(8,128)S(1)}, bf16[8,256,256]{2,1,0:T(8,128)(2,1)S(1)}) custom-call(s32[17]{0:T(128)S(1)} %pad_add_fusion.refs_0_, bf16[4,64,128]{2,1,0:T(8,128)(2,1)S(1)} %pad_maximum_fusion.1.refs_1_, bf16[4,64,128]{2,1,0:T(8,128)(2,1)S(1)} %collective-permute-done.3.refs_2_, bf16[4,64,128]{2,1,0:T(8,128)(2,1)S(1)} %collective-permute-done.4.refs_3_, ...), custom_call_target="tpu_custom_call" | custom-call | tf_op jit(solution)/shard_map/pallas_call | solution.py:192
  48.7 10.3 %shard_map.69.refs_3_ = f32[16,72,128]{2,1,0:T(8,128)S(1)} custom-call(s32[17]{0:T(128)S(1)} %pad_add_fusion.refs_0_, bf16[8,256,256]{2,1,0:T(8,128)(2,1)S(1)} %get-tuple-element.9.refs_1_, bf16[8,264,128]{2,1,0:T(8,128)(2,1)S(1)} %all_to_all.25.refs_2_, f32[16,72,128]{2,1,0:T(8,128)S(1)} %get-tuple-element.11.refs_3_), custom_call_target="tpu_custom_call" | custom-call | tf_op jit(solution)/shard_map/pallas_call | solution.py:192
  59.1 10.3 %shard_map.70 = f32[16,72,128]{2,1,0:T(8,128)S(1)} custom-call(s32[17]{0:T(128)S(1)} %pad_add_fusion.refs_0_, bf16[8,256,256]{2,1,0:T(8,128)(2,1)S(1)} %get-tuple-element.9.refs_1_, bf16[8,264,128]{2,1,0:T(8,128)(2,1)S(1)} %collective-permute-done.7.refs_2_, f32[16,72,128]{2,1,0:T(8,128)S(1)} %shard_map.69.refs_3_), custom_call_target="tpu_custom_call" | custom-call | tf_op jit(solution)/shard_map/pallas_call | solution.py:192
  69.4 16.6 %all_to_all.26.got_ref = f32[16,72,128]{2,1,0:T(8,128)S(1)} all-to-all(f32[16,72,128]{2,1,0:T(8,128)S(1)} %shard_map.70), channel_id=1, replica_groups=mesh['yl'=2,'z'=8,'yh'=2,'x'=4,'core'=2] {'yl','yh','x'}, dimensions={0} | all-to-all | bytes 1179648 | tf_op jit(solution)/shard_map/all_to_all | solution.py:317
  86.0 1.0 moments.1
  87.0 4.8 %all-to-all-start.2 = ((f32[16,8,256]{2,1,0:T(8,128)}), f32[16,8,256]{2,1,0:T(8,128)S(1)}, u32[]{:S(2)}, u32[]{:S(2)}) async-start(f32[16,8,256]{2,1,0:T(8,128)} %get-tuple-element.13), calls=%async_computation.2 | async-start | bytes 262144 | tf_op jit(solution)/shard_map/all_to_all | solution.py:317
  92.2 6.4 %all-to-all-done.2 = f32[16,8,256]{2,1,0:T(8,128)S(1)} async-done(((f32[16,8,256]{2,1,0:T(8,128)}), f32[16,8,256]{2,1,0:T(8,128)S(1)}, u32[]{:S(2)}, u32[]{:S(2)}) %all-to-all-start.2) | async-done | bytes 131104 | tf_op jit(solution)/shard_map/all_to_all | solution.py:317
  99.2 3.5 %all-to-all-start.3 = ((f32[16,8,256]{2,1,0:T(8,128)}), f32[16,8,256]{2,1,0:T(8,128)S(1)}, u32[]{:S(2)}, u32[]{:S(2)}) async-start(f32[16,8,256]{2,1,0:T(8,128)} %broadcast_in_dim.24), calls=%async_computation.3 | async-start | bytes 262144 | tf_op jit(solution)/shard_map/all_to_all | solution.py:317
  102.9 8.4 %all-to-all-done.3 = f32[16,8,256]{2,1,0:T(8,128)S(1)} async-done(((f32[16,8,256]{2,1,0:T(8,128)}), f32[16,8,256]{2,1,0:T(8,128)S(1)}, u32[]{:S(2)}, u32[]{:S(2)}) %all-to-all-start.3) | async-done | bytes 131104 | tf_op jit(solution)/shard_map/all_to_all | solution.py:317
  112.1 4.8 %all-to-all-start.4 = ((f32[16,8,256]{2,1,0:T(8,128)}), f32[16,8,256]{2,1,0:T(8,128)S(1)}, u32[]{:S(2)}, u32[]{:S(2)}) async-start(f32[16,8,256]{2,1,0:T(8,128)} %broadcast_in_dim.25), calls=%async_computation.4 | async-start | bytes 262144 | tf_op jit(solution)/shard_map/all_to_all | solution.py:317
  117.5 6.6 %all-to-all-done.4.sums_ref = f32[16,8,256]{2,1,0:T(8,128)S(1)} async-done(((f32[16,8,256]{2,1,0:T(8,128)}), f32[16,8,256]{2,1,0:T(8,128)S(1)}, u32[]{:S(2)}, u32[]{:S(2)}) %all-to-all-start.4) | async-done | bytes 131104 | tf_op jit(solution)/shard_map/all_to_all | solution.py:317
  124.1 1.9 %correlate.1 = f32[2000,256]{1,0:T(8,128)} custom-call(f32[16,8,256]{2,1,0:T(8,128)S(1)} %all-to-all-done.4.sums_ref, bf16[2000,256]{1,0:T(8,128)(2,1)S(1)} %pad_maximum_fusion.split_ref), custom_call_target="tpu_custom_call" | custom-call | tf_op jit(solution)/shard_map/correlate/pallas_call | solution.py:292
  (25 shorter events, 3.7 us)
Async XLA Ops:
  1.3 0.8 copy-start
  28.3 30.7 %collective-permute-start.7 = (bf16[8,264,128]{2,1,0:T(8,128)(2,1)S(1)}, bf16[8,264,128]{2,1,0:T(8,128)(2,1)S(1)}, u32[]{:S(2)}, u32[]{:S(2)}) collective-permute-start(bf16[8,264,128]{2,1,0:T(8,128)(2,1)S(1)} %all_to_all.25.refs_2_), channel_id=1, source_target_pairs={{0,1},{1,0},{2,3},{3,2},{4,5},{5,4},{6,7},{7,6},{8,9},{9,8},{10,11... | collective-permute-start | bytes 1622024 | tf_op jit(solution)/shard_map/ppermute | solution.py:344
  28.3 4.8 %collective-permute-start = (bf16[64,128]{1,0:T(8,128)(2,1)}, bf16[64,128]{1,0:T(8,128)(2,1)S(1)}, u32[]{:S(2)}, u32[]{:S(2)}) collective-permute-start(bf16[64,128]{1,0:T(8,128)(2,1)} %x_ref.1), channel_id=1, source_target_pairs={{0,2},{2,4},{4,6},{6,0},{1,3},{3,5},{5,7},{7,1},{8,10},{10,12},{12... | collective-permute-start | bytes 49160 | tf_op jit(solution)/shard_map/ppermute | solution.py:335
  29.8 5.5 %collective-permute-start.1 = (bf16[64,128]{1,0:T(8,128)(2,1)}, bf16[64,128]{1,0:T(8,128)(2,1)S(1)}, u32[]{:S(2)}, u32[]{:S(2)}) collective-permute-start(bf16[64,128]{1,0:T(8,128)(2,1)} %x_ref.1), channel_id=1, source_target_pairs={{0,4},{2,6},{4,0},{6,2},{1,5},{3,7},{5,1},{7,3},{8,12},{10,14},{12... | collective-permute-start | bytes 49160 | tf_op jit(solution)/shard_map/ppermute | solution.py:335
  31.0 4.3 %collective-permute-start.2 = (bf16[64,128]{1,0:T(8,128)(2,1)}, bf16[64,128]{1,0:T(8,128)(2,1)S(1)}, u32[]{:S(2)}, u32[]{:S(2)}) collective-permute-start(bf16[64,128]{1,0:T(8,128)(2,1)} %x_ref.1), channel_id=1, source_target_pairs={{0,6},{2,0},{4,2},{6,4},{1,7},{3,1},{5,3},{7,5},{8,14},{10,8},{12,... | collective-permute-start | bytes 49160 | tf_op jit(solution)/shard_map/ppermute | solution.py:335
  33.1 8.9 %collective-permute-start.6 = (bf16[1,264,128]{2,1,0:T(8,128)(2,1)S(1)}, bf16[1,264,128]{2,1,0:T(8,128)(2,1)S(1)}, u32[]{:S(2)}, u32[]{:S(2)}) collective-permute-start(bf16[1,264,128]{2,1,0:T(8,128)(2,1)S(1)} %get-tuple-element.8.refs_5_), channel_id=1, source_target_pairs={{0,1},{1,0},{2,3},{3,2},{4,5},{5,4},{6,7},{7,6},{8,9},{9,8},{10,11... | collective-permute-start | bytes 202760 | tf_op jit(solution)/shard_map/ppermute | solution.py:334
  36.0 6.3 %collective-permute-start.3 = (bf16[4,64,128]{2,1,0:T(8,128)(2,1)S(1)}, bf16[4,64,128]{2,1,0:T(8,128)(2,1)S(1)}, u32[]{:S(2)}, u32[]{:S(2)}) collective-permute-start(bf16[4,64,128]{2,1,0:T(8,128)(2,1)S(1)} %pad_maximum_fusion.1.refs_1_), channel_id=1, source_target_pairs={{0,128},{128,8},{8,136},{136,0},{1,129},{129,9},{9,137},{137,1},{2... | collective-permute-start | bytes 196616 | tf_op jit(solution)/shard_map/ppermute | solution.py:337
  37.7 5.8 %collective-permute-start.4 = (bf16[4,64,128]{2,1,0:T(8,128)(2,1)S(1)}, bf16[4,64,128]{2,1,0:T(8,128)(2,1)S(1)}, u32[]{:S(2)}, u32[]{:S(2)}) collective-permute-start(bf16[4,64,128]{2,1,0:T(8,128)(2,1)S(1)} %pad_maximum_fusion.1.refs_1_), channel_id=1, source_target_pairs={{0,8},{128,136},{8,0},{136,128},{1,9},{129,137},{9,1},{137,129},{2... | collective-permute-start | bytes 196616 | tf_op jit(solution)/shard_map/ppermute | solution.py:337
  40.6 4.3 %collective-permute-start.5 = (bf16[4,64,128]{2,1,0:T(8,128)(2,1)S(1)}, bf16[4,64,128]{2,1,0:T(8,128)(2,1)S(1)}, u32[]{:S(2)}, u32[]{:S(2)}) collective-permute-start(bf16[4,64,128]{2,1,0:T(8,128)(2,1)S(1)} %pad_maximum_fusion.1.refs_1_), channel_id=1, source_target_pairs={{0,136},{128,0},{8,128},{136,8},{1,137},{129,1},{9,129},{137,9},{2... | collective-permute-start | bytes 196616 | tf_op jit(solution)/shard_map/ppermute | solution.py:337
  59.0 27.0 %copy-start.1 = (bf16[64,128]{1,0:T(8,128)(2,1)S(1)}, bf16[64,128]{1,0:T(8,128)(2,1)}, u32[]{:S(2)}) copy-start(bf16[64,128]{1,0:T(8,128)(2,1)} %x_ref.1) | copy-start | bytes 49156
  59.1 27.0 %copy-start.2 = (s32[128]{0:T(128)S(1)}, s32[128]{0:T(128)}, u32[]{:S(2)}) copy-start(s32[128]{0:T(128)} %param.8) | copy-start | bytes 1540
  59.1 32.8 %copy-start.3 = (f32[64,2000]{1,0:T(8,128)S(1)}, f32[64,2000]{1,0:T(8,128)}, u32[]{:S(2)}) copy-start(f32[64,2000]{1,0:T(8,128)} %param.9) | copy-start | bytes 1536004
  87.0 11.5 %all-to-all-start.2 = ((f32[16,8,256]{2,1,0:T(8,128)}), f32[16,8,256]{2,1,0:T(8,128)S(1)}, u32[]{:S(2)}, u32[]{:S(2)}) async-start(f32[16,8,256]{2,1,0:T(8,128)} %get-tuple-element.13), calls=%async_computation.2 | async-start | bytes 262144 | tf_op jit(solution)/shard_map/all_to_all | solution.py:317
  99.2 12.1 %all-to-all-start.3 = ((f32[16,8,256]{2,1,0:T(8,128)}), f32[16,8,256]{2,1,0:T(8,128)S(1)}, u32[]{:S(2)}, u32[]{:S(2)}) async-start(f32[16,8,256]{2,1,0:T(8,128)} %broadcast_in_dim.24), calls=%async_computation.3 | async-start | bytes 262144 | tf_op jit(solution)/shard_map/all_to_all | solution.py:317
  112.1 12.1 %all-to-all-start.4 = ((f32[16,8,256]{2,1,0:T(8,128)}), f32[16,8,256]{2,1,0:T(8,128)S(1)}, u32[]{:S(2)}, u32[]{:S(2)}) async-start(f32[16,8,256]{2,1,0:T(8,128)} %broadcast_in_dim.25), calls=%async_computation.4 | async-start | bytes 262144 | tf_op jit(solution)/shard_map/all_to_all | solution.py:317

commit v4 on v3

--- a/solution.py
+++ b/solution.py
@@ -25,6 +25,8 @@
 EARLY_GROUP = ("yl", "yh", "x")
 LATE_GROUP = ("z", "core")
 
+Z_STEPS = (1, 7, 2, 6, 3, 5, 4)
+
 
 def split3(v):
     high = v.astype(bf16).astype(f32)
@@ -39,35 +41,28 @@
     return base
 
 
-def pack_kernel(late_ref, log_ref, one_ref, all_ref):
+def pack_kernel(late_ref, log_ref, out_ref):
     cells = late_ref.shape[1]
     blocks = [late_ref[:, 128 * k : 128 * (k + 1)] for k in range(cells // 128)]
     logs = [log_ref[:, 128 * k : 128 * (k + 1)].astype(f32) for k in range(cells // 128)]
     tail = jnp.concatenate(logs + [jnp.zeros((8 - cells // 128, 128), f32)], 0).astype(bf16)
-    one = jnp.concatenate(blocks + [tail], 0)
-    one_ref[0] = one
-    for k in range(all_ref.shape[0]):
-        all_ref[k] = one
-
-
-def pack(late, logs, copies):
+    out_ref[0] = jnp.concatenate(blocks + [tail], 0)
+
+
+def pack(late, logs):
     rows = DIM * late.shape[1] // 128 + 8
     return pl.pallas_call(
         pack_kernel,
-        out_shape=(
-            jax.ShapeDtypeStruct((1, rows, 128), bf16),
-            jax.ShapeDtypeStruct((copies, rows, 128), bf16),
-        ),
+        out_shape=jax.ShapeDtypeStruct((1, rows, 128), bf16),
         in_specs=[pl.BlockSpec(memory_space=pltpu.VMEM)] * 2,
-        out_specs=(pl.BlockSpec(memory_space=pltpu.VMEM),) * 2,
+        out_specs=pl.BlockSpec(memory_space=pltpu.VMEM),
         compiler_params=pltpu.CompilerParams(vmem_limit_bytes=8 * 2**20),
         name="pack",
     )(late, logs[None])
 
 
-def attention_kernel(*refs, n_x, n_late, skip, tile, parts, has_state):
+def attention_kernel(*refs, n_x, n_late, tile, score_parts, parts, has_state):
     refs = list(refs)
-    slot_ref = refs.pop(0)
     x_refs = [refs.pop(0) for _ in range(n_x)]
     late_refs = [refs.pop(0) for _ in range(n_late)]
     if has_state:
@@ -80,8 +75,7 @@
     pairs = xa.shape[0]
     chunk = (late_refs[0].shape[1] - 8) * 2
     groups = chunk // 128
-    chunks = sum(r.shape[0] - skip for r in late_refs)
-    tiles = chunks * chunk // tile
+    tiles = n_late * chunk // tile
 
     if not has_state:
         row = lax.broadcasted_iota(jnp.int32, (DIM, wide), 0)
@@ -112,19 +106,8 @@
         ones = jnp.where(lax.broadcasted_iota(jnp.int32, (16, chunk), 0) == 0, 1.0, 0.0)
         yw[:, pl.ds(first, chunk)] = jnp.concatenate([yb, ones.astype(bf16)], 0)
 
-    if skip:
-        here = slot_ref[2 * pairs]
-        count = late_refs[0].shape[0]
-
-        def prepare(j, carry):
-            for k, ref in enumerate(late_refs):
-                prepare_late(ref, (here + 1 + j) % count, k * (count - 1) + j)
-            return carry
-
-        lax.fori_loop(0, count - 1, prepare, 0)
-    else:
-        for k, ref in enumerate(late_refs):
-            prepare_late(ref, 0, k)
+    for k, ref in enumerate(late_refs):
+        prepare_late(ref, 0, k)
     acc[...] = jnp.zeros_like(acc)
 
     def score_part(pair, first, offset, size, slot, top):
@@ -135,8 +118,9 @@
 
     steps = pairs * tiles
     spans = [(sum(parts[:k]), parts[k]) for k in range(len(parts))]
+    score_spans = [(sum(score_parts[:k]), score_parts[k]) for k in range(len(score_parts))]
     top = None
-    for offset, size in spans:
+    for offset, size in score_spans:
         top = score_part(0, 0, offset, size, 0, top)
     mbuf[0] = top
 
@@ -146,7 +130,7 @@
         following = jnp.minimum(n + 1, steps - 1)
         next_first = pl.multiple_of((following % tiles) * tile, tile)
         fresh = n % tiles == 0
-        left, right = slot_ref[2 * pair], slot_ref[2 * pair + 1]
+        left, right = 2 * pair, 2 * pair + 1
         carried = acc[...]
         if has_state:
             state = jnp.concatenate([state_ref[left], state_ref[right]], 1)
@@ -158,8 +142,11 @@
         shrink = jnp.exp2(before - now)
         top = None
         sums = None
+        left_over = list(score_spans)
         for offset, size in spans:
-            top = score_part(following // tiles, next_first, offset, size, 1 - slot, top)
+            while left_over and left_over[0][0] <= offset:
+                span = left_over.pop(0)
+                top = score_part(following // tiles, next_first, *span, 1 - slot, top)
             weights = jnp.exp2(sbuf[slot, offset : offset + size, :] - now).astype(bf16)
             more = jnp.dot(yw[:, pl.ds(first + offset, size)], weights, preferred_element_type=f32)
             sums = more if sums is None else sums + more
@@ -178,10 +165,10 @@
     lax.fori_loop(0, steps // 2, two_steps, jnp.full((1, wide), LOWEST, f32))
 
 
-def attention(slots, early, late, state=None, skip=0, tile=1024, parts=(512, 512)):
+def attention(early, late, state=None, tile=1024, score_parts=(512, 512), parts=(512, 512)):
     wide = 256
     pairs = early[0].shape[0] if state is not None else sum(e.shape[0] for e in early) // 2
-    late_total = sum(r.shape[0] - skip for r in late) * (late[0].shape[1] - 8) * 2
+    late_total = len(late) * (late[0].shape[1] - 8) * 2
     out_shape = [jax.ShapeDtypeStruct((2 * pairs, 72, 128), f32)]
     operands = list(early) + list(late)
     if state is None:
@@ -194,13 +181,13 @@
             attention_kernel,
             n_x=len(early),
             n_late=len(late),
-            skip=skip,
             tile=tile,
+            score_parts=score_parts,
             parts=parts,
             has_state=state is not None,
         ),
         out_shape=out_shape,
-        in_specs=[pl.BlockSpec(memory_space=pltpu.SMEM)] + [vmem] * len(operands),
+        in_specs=[vmem] * len(operands),
         out_specs=[vmem] * len(out_shape),
         scratch_shapes=[
             pltpu.VMEM((late_total, 256), bf16),
@@ -210,7 +197,7 @@
             pltpu.VMEM((72, wide), f32),
         ],
         compiler_params=pltpu.CompilerParams(vmem_limit_bytes=32 * 2**20),
-    )(slots, *operands)
+    )(*operands)
 
 
 def moments_kernel(got_ref, x_ref, label_ref, projected_ref, sums_ref):
@@ -308,11 +295,6 @@
     return [(i, (i + k) % n) for i in range(n)]
 
 
-def shift_y(k):
-    place = [y % 2 * 2 + y // 2 for y in range(4)]
-    return [(place[y], place[(y + k) % 4]) for y in range(4)]
-
-
 def exchange(blocks, axes):
     return lax.all_to_all(blocks, axes, 0, 0, tiled=False)
 
@@ -328,23 +310,18 @@
     low = turned - high
     split = jnp.concatenate([high, low, high, low], 1).astype(bf16)
 
-    late_one, late_copies = pack(late, late_logs, SIZES[1])
-    late_own = exchange(late_copies, "z")
+    early_all = spread(early, EARLY_GROUP)
+    late_one = pack(late, late_logs)
     swap = [(0, 1), (1, 0)]
     late_near = lax.ppermute(late_one, "core", swap)
-    line = [early] + [lax.ppermute(early, "x", shift(4, k)) for k in range(1, 4)]
-    line = jnp.stack(line)
-    early_all = [line] + [lax.ppermute(line, ("yl", "yh"), shift_y(k)) for k in range(1, 4)]
-    y, x = 2 * lax.axis_index("yh") + lax.axis_index("yl"), lax.axis_index("x")
-    back = jnp.arange(16, dtype=jnp.int32)
-    to_y, to_x = (y - back // 4) % 4, (x - back % 4) % 4
-    slots = to_y % 2 * 8 + to_y // 2 * 4 + to_x
-    slots = jnp.concatenate([slots, lax.axis_index("z")[None]]).astype(jnp.int32)
-    partial, prepared = attention(slots, early_all, [late_one, late_near])
-    late_other = lax.ppermute(late_own, "core", swap)
-    rest = dict(skip=1, tile=1792, parts=(512, 512, 512, 256))
-    (partial,) = attention(slots, [prepared], [late_own], partial, **rest)
-    (partial,) = attention(slots, [prepared], [late_other], partial, **rest)
+    late_far = []
+    for k in Z_STEPS:
+        own = lax.ppermute(late_one, "z", shift(SIZES[1], k))
+        late_far += [own, lax.ppermute(own, "core", swap)]
+    partial, prepared = attention([early_all], [late_one, late_near])
+    (partial,) = attention(
+        [prepared], late_far, partial, tile=3584, score_parts=(512,) * 7, parts=(512,) * 7
+    )
     got = exchange(partial, EARLY_GROUP)
     projected, sums = moments(got, early, labels[None])
     sums = jnp.sum(exchange(sums, EARLY_GROUP), 0)

time: 128 us -> 118 us (0.922)
  the two profiles are of different devices: /device:TPU:2 before, /device:TPU:1 now
where the time goes in v4:
time: 118 us
  starting transfers between devices  48.5 us (41%)
  Pallas kernels  22.3 us (19%)
  waiting for transfers between devices  22 us (19%)
  blocking collectives  18.2 us (15%)
  local copies, waits for them, and re-layouts  4.67 us (4%)
    all_to_all x4, starting transfers between devices, exchange(): return lax.all_to_all(blocks, axes, 0, 0, tiled=False)  22.8 us
    all_to_all x4, waiting for transfers between devices, exchange(): return lax.all_to_all(blocks, axes, 0, 0, tiled=False)  21.9 us
    pallas_call x2, Pallas kernels, attention(): pl.pallas_call(functools.partial(attention_kernel, n_x=len(early), n_late...  19.4 us
    all_to_all x1, blocking collectives, exchange(): return lax.all_to_all(blocks, axes, 0, 0, tiled=False)  18.2 us
    ppermute x7, starting transfers between devices, program(): own = lax.ppermute(late_one, 'z', shift(SIZES[1], k))  17.6 us
    ppermute x7, starting transfers between devices, program(): late_far += [own, lax.ppermute(own, 'core', swap)]  6.98 us
    broadcast_in_dim x3, local copies, waits for them, and re-layouts, spread(): return exchange(jnp.broadcast_to(block[None], (16,) + block.shape), axes)  2.8 us
  transfers between devices with their start and end apart: 19, of which 3 were waited for; matrix products, arithmetic and copies ran while one was open for 2% of the time, Pallas kernels for 3%

profile of v4, /device:TPU:1, one launch (start us, length us, event | category | flops | bytes accessed | tf_op | source)
XLA Modules:
  0.0 117.5 jit_solution(16455233333722498894)
XLA Ops:
  0.6 1.5 %broadcast_in_dim.10 = bf16[16,64,128]{2,1,0:T(8,128)(2,1)} broadcast(bf16[64,128]{1,0:T(8,128)(2,1)} %x_ref.1), dimensions={1,2} | broadcast | bytes 278528 | tf_op jit(solution)/shard_map/broadcast_in_dim | solution.py:303
  2.1 7.6 %all-to-all-start = ((bf16[16,64,128]{2,1,0:T(8,128)(2,1)}), bf16[16,64,128]{2,1,0:T(8,128)(2,1)S(1)}, u32[]{:S(2)}, u32[]{:S(2)}) async-start(bf16[16,64,128]{2,1,0:T(8,128)(2,1)} %broadcast_in_dim.10), calls=%async_computation | async-start | bytes 524288 | tf_op jit(solution)/shard_map/all_to_all | solution.py:299
  10.4 0.8 copy-done.1
  11.2 1.0 collective-permute-start
  12.3 1.6 %collective-permute-start.1 = (bf16[1,264,128]{2,1,0:T(8,128)(2,1)S(1)}, bf16[1,264,128]{2,1,0:T(8,128)(2,1)S(1)}, u32[]{:S(2)}, u32[]{:S(2)}) collective-permute-start(bf16[1,264,128]{2,1,0:T(8,128)(2,1)S(1)} %pack.1.refs_1_), channel_id=1, source_target_pairs={{0,16},{16,32},{32,48},{48,64},{64,80},{80,96},{96,112},{112,0},{1... | collective-permute-start | bytes 202760 | tf_op jit(solution)/shard_map/ppermute | solution.py:319
  13.9 3.9 %collective-permute-start.3 = (bf16[1,264,128]{2,1,0:T(8,128)(2,1)S(1)}, bf16[1,264,128]{2,1,0:T(8,128)(2,1)S(1)}, u32[]{:S(2)}, u32[]{:S(2)}) collective-permute-start(bf16[1,264,128]{2,1,0:T(8,128)(2,1)S(1)} %pack.1.refs_1_), channel_id=1, source_target_pairs={{0,112},{16,0},{32,16},{48,32},{64,48},{80,64},{96,80},{112,96},{1... | collective-permute-start | bytes 202760 | tf_op jit(solution)/shard_map/ppermute | solution.py:319
  17.9 3.6 %collective-permute-start.7 = (bf16[1,264,128]{2,1,0:T(8,128)(2,1)S(1)}, bf16[1,264,128]{2,1,0:T(8,128)(2,1)S(1)}, u32[]{:S(2)}, u32[]{:S(2)}) collective-permute-start(bf16[1,264,128]{2,1,0:T(8,128)(2,1)S(1)} %pack.1.refs_1_), channel_id=1, source_target_pairs={{0,96},{16,112},{32,0},{48,16},{64,32},{80,48},{96,64},{112,80},{1... | collective-permute-start | bytes 202760 | tf_op jit(solution)/shard_map/ppermute | solution.py:319
  21.8 4.1 %collective-permute-start.11 = (bf16[1,264,128]{2,1,0:T(8,128)(2,1)S(1)}, bf16[1,264,128]{2,1,0:T(8,128)(2,1)S(1)}, u32[]{:S(2)}, u32[]{:S(2)}) collective-permute-start(bf16[1,264,128]{2,1,0:T(8,128)(2,1)S(1)} %pack.1.refs_1_), channel_id=1, source_target_pairs={{0,80},{16,96},{32,112},{48,0},{64,16},{80,32},{96,48},{112,64},{1... | collective-permute-start | bytes 202760 | tf_op jit(solution)/shard_map/ppermute | solution.py:319
  25.9 4.0 %collective-permute-start.13 = (bf16[1,264,128]{2,1,0:T(8,128)(2,1)S(1)}, bf16[1,264,128]{2,1,0:T(8,128)(2,1)S(1)}, u32[]{:S(2)}, u32[]{:S(2)}) collective-permute-start(bf16[1,264,128]{2,1,0:T(8,128)(2,1)S(1)} %pack.1.refs_1_), channel_id=1, source_target_pairs={{0,64},{16,80},{32,96},{48,112},{64,0},{80,16},{96,32},{112,48},{1... | collective-permute-start | bytes 202760 | tf_op jit(solution)/shard_map/ppermute | solution.py:319
  29.9 2.1 %collective-permute-start.2 = (bf16[1,264,128]{2,1,0:T(8,128)(2,1)S(1)}, bf16[1,264,128]{2,1,0:T(8,128)(2,1)S(1)}, u32[]{:S(2)}, u32[]{:S(2)}) collective-permute-start(bf16[1,264,128]{2,1,0:T(8,128)(2,1)S(1)} %collective-permute-done.1.refs_1_), channel_id=1, source_target_pairs={{0,1},{1,0},{2,3},{3,2},{4,5},{5,4},{6,7},{7,6},{8,9},{9,8},{10,11... | collective-permute-start | bytes 202760 | tf_op jit(solution)/shard_map/ppermute | solution.py:320
  32.5 1.1 collective-permute-start.8
  33.6 2.8 %collective-permute-start.10 = (bf16[1,264,128]{2,1,0:T(8,128)(2,1)S(1)}, bf16[1,264,128]{2,1,0:T(8,128)(2,1)S(1)}, u32[]{:S(2)}, u32[]{:S(2)}) collective-permute-start(bf16[1,264,128]{2,1,0:T(8,128)(2,1)S(1)} %collective-permute-done.9.refs_9_), channel_id=1, source_target_pairs={{0,1},{1,0},{2,3},{3,2},{4,5},{5,4},{6,7},{7,6},{8,9},{9,8},{10,11... | collective-permute-start | bytes 202760 | tf_op jit(solution)/shard_map/ppermute | solution.py:320
  36.9 3.3 %shard_map.68 = (f32[16,72,128]{2,1,0:T(8,128)S(1)}, bf16[8,256,256]{2,1,0:T(8,128)(2,1)S(1)}) custom-call(bf16[16,64,128]{2,1,0:T(8,128)(2,1)S(1)} %all-to-all-done.refs_0_, bf16[1,264,128]{2,1,0:T(8,128)(2,1)S(1)} %pack.1.refs_1_, bf16[1,264,128]{2,1,0:T(8,128)(2,1)S(1)} %collective-permute-done.refs_2_), custom_call_target="tpu_custom_call" | custom-call | tf_op jit(solution)/shard_map/pallas_call | solution.py:179
  40.3 16.1 %shard_map.69 = f32[16,72,128]{2,1,0:T(8,128)S(1)} custom-call(bf16[8,256,256]{2,1,0:T(8,128)(2,1)S(1)} %get-tuple-element.6.refs_0_, bf16[1,264,128]{2,1,0:T(8,128)(2,1)S(1)} %collective-permute-done.1.refs_1_, bf16[1,264,128]{2,1,0:T(8,128)(2,1)S(1)} %collective-permute-done.2.refs_2_, bf16[1,264,128]{2,1,0:T(8,128)(2,1)S(1)} %collective-permute-done.3.refs_3_, ...), custom_call_target="tpu_custom_call" | custom-call | tf_op jit(solution)/shard_map/pallas_call | solution.py:179
  56.4 18.2 %all_to_all.25.got_ref = f32[16,72,128]{2,1,0:T(8,128)S(1)} all-to-all(f32[16,72,128]{2,1,0:T(8,128)S(1)} %shard_map.69), channel_id=1, replica_groups=mesh['yl'=2,'z'=8,'yh'=2,'x'=4,'core'=2] {'yl','yh','x'}, dimensions={0} | all-to-all | bytes 1179648 | tf_op jit(solution)/shard_map/all_to_all | solution.py:299
  74.6 1.0 moments.1
  75.6 3.5 %all-to-all-start.2 = ((f32[16,8,256]{2,1,0:T(8,128)}), f32[16,8,256]{2,1,0:T(8,128)S(1)}, u32[]{:S(2)}, u32[]{:S(2)}) async-start(f32[16,8,256]{2,1,0:T(8,128)} %get-tuple-element.9), calls=%async_computation.2 | async-start | bytes 262144 | tf_op jit(solution)/shard_map/all_to_all | solution.py:299
  79.5 6.5 %all-to-all-done.2 = f32[16,8,256]{2,1,0:T(8,128)S(1)} async-done(((f32[16,8,256]{2,1,0:T(8,128)}), f32[16,8,256]{2,1,0:T(8,128)S(1)}, u32[]{:S(2)}, u32[]{:S(2)}) %all-to-all-start.2) | async-done | bytes 131104 | tf_op jit(solution)/shard_map/all_to_all | solution.py:299
  86.6 8.2 %all-to-all-start.3 = ((f32[16,8,256]{2,1,0:T(8,128)}), f32[16,8,256]{2,1,0:T(8,128)S(1)}, u32[]{:S(2)}, u32[]{:S(2)}) async-start(f32[16,8,256]{2,1,0:T(8,128)} %broadcast_in_dim.13), calls=%async_computation.3 | async-start | bytes 262144 | tf_op jit(solution)/shard_map/all_to_all | solution.py:299
  95.0 8.7 %all-to-all-done.3 = f32[16,8,256]{2,1,0:T(8,128)S(1)} async-done(((f32[16,8,256]{2,1,0:T(8,128)}), f32[16,8,256]{2,1,0:T(8,128)S(1)}, u32[]{:S(2)}, u32[]{:S(2)}) %all-to-all-start.3) | async-done | bytes 131104 | tf_op jit(solution)/shard_map/all_to_all | solution.py:299
  104.4 3.5 %all-to-all-start.4 = ((f32[16,8,256]{2,1,0:T(8,128)}), f32[16,8,256]{2,1,0:T(8,128)S(1)}, u32[]{:S(2)}, u32[]{:S(2)}) async-start(f32[16,8,256]{2,1,0:T(8,128)} %broadcast_in_dim.28), calls=%async_computation.4 | async-start | bytes 262144 | tf_op jit(solution)/shard_map/all_to_all | solution.py:299
  107.9 0.7 pad_maximum_fusion.split_ref
  108.7 6.8 %all-to-all-done.4.sums_ref = f32[16,8,256]{2,1,0:T(8,128)S(1)} async-done(((f32[16,8,256]{2,1,0:T(8,128)}), f32[16,8,256]{2,1,0:T(8,128)S(1)}, u32[]{:S(2)}, u32[]{:S(2)}) %all-to-all-start.4) | async-done | bytes 131104 | tf_op jit(solution)/shard_map/all_to_all | solution.py:299
  115.4 1.9 %correlate.1 = f32[2000,256]{1,0:T(8,128)} custom-call(f32[16,8,256]{2,1,0:T(8,128)S(1)} %all-to-all-done.4.sums_ref, bf16[2000,256]{1,0:T(8,128)(2,1)S(1)} %pad_maximum_fusion.split_ref), custom_call_target="tpu_custom_call" | custom-call | tf_op jit(solution)/shard_map/correlate/pallas_call | solution.py:279
  (37 shorter events, 4.1 us)
Async XLA Ops:
  2.1 34.8 %all-to-all-start = ((bf16[16,64,128]{2,1,0:T(8,128)(2,1)}), bf16[16,64,128]{2,1,0:T(8,128)(2,1)S(1)}, u32[]{:S(2)}, u32[]{:S(2)}) async-start(bf16[16,64,128]{2,1,0:T(8,128)(2,1)} %broadcast_in_dim.10), calls=%async_computation | async-start | bytes 524288 | tf_op jit(solution)/shard_map/all_to_all | solution.py:299
  10.4 0.8 copy-start.1
  11.2 10.2 %collective-permute-start = (bf16[1,264,128]{2,1,0:T(8,128)(2,1)S(1)}, bf16[1,264,128]{2,1,0:T(8,128)(2,1)S(1)}, u32[]{:S(2)}, u32[]{:S(2)}) collective-permute-start(bf16[1,264,128]{2,1,0:T(8,128)(2,1)S(1)} %pack.1.refs_1_), channel_id=1, source_target_pairs={{0,1},{1,0},{2,3},{3,2},{4,5},{5,4},{6,7},{7,6},{8,9},{9,8},{10,11... | collective-permute-start | bytes 202760 | tf_op jit(solution)/shard_map/ppermute | solution.py:316
  12.3 9.6 %collective-permute-start.1 = (bf16[1,264,128]{2,1,0:T(8,128)(2,1)S(1)}, bf16[1,264,128]{2,1,0:T(8,128)(2,1)S(1)}, u32[]{:S(2)}, u32[]{:S(2)}) collective-permute-start(bf16[1,264,128]{2,1,0:T(8,128)(2,1)S(1)} %pack.1.refs_1_), channel_id=1, source_target_pairs={{0,16},{16,32},{32,48},{48,64},{64,80},{80,96},{96,112},{112,0},{1... | collective-permute-start | bytes 202760 | tf_op jit(solution)/shard_map/ppermute | solution.py:319
  13.9 12.0 %collective-permute-start.3 = (bf16[1,264,128]{2,1,0:T(8,128)(2,1)S(1)}, bf16[1,264,128]{2,1,0:T(8,128)(2,1)S(1)}, u32[]{:S(2)}, u32[]{:S(2)}) collective-permute-start(bf16[1,264,128]{2,1,0:T(8,128)(2,1)S(1)} %pack.1.refs_1_), channel_id=1, source_target_pairs={{0,112},{16,0},{32,16},{48,32},{64,48},{80,64},{96,80},{112,96},{1... | collective-permute-start | bytes 202760 | tf_op jit(solution)/shard_map/ppermute | solution.py:319
  17.9 12.1 %collective-permute-start.5 = (bf16[1,264,128]{2,1,0:T(8,128)(2,1)S(1)}, bf16[1,264,128]{2,1,0:T(8,128)(2,1)S(1)}, u32[]{:S(2)}, u32[]{:S(2)}) collective-permute-start(bf16[1,264,128]{2,1,0:T(8,128)(2,1)S(1)} %pack.1.refs_1_), channel_id=1, source_target_pairs={{0,32},{16,48},{32,64},{48,80},{64,96},{80,112},{96,0},{112,16},{1... | collective-permute-start | bytes 202760 | tf_op jit(solution)/shard_map/ppermute | solution.py:319
  17.9 14.1 %collective-permute-start.7 = (bf16[1,264,128]{2,1,0:T(8,128)(2,1)S(1)}, bf16[1,264,128]{2,1,0:T(8,128)(2,1)S(1)}, u32[]{:S(2)}, u32[]{:S(2)}) collective-permute-start(bf16[1,264,128]{2,1,0:T(8,128)(2,1)S(1)} %pack.1.refs_1_), channel_id=1, source_target_pairs={{0,96},{16,112},{32,0},{48,16},{64,32},{80,48},{96,64},{112,80},{1... | collective-permute-start | bytes 202760 | tf_op jit(solution)/shard_map/ppermute | solution.py:319
  21.4 10.6 %collective-permute-start.9 = (bf16[1,264,128]{2,1,0:T(8,128)(2,1)S(1)}, bf16[1,264,128]{2,1,0:T(8,128)(2,1)S(1)}, u32[]{:S(2)}, u32[]{:S(2)}) collective-permute-start(bf16[1,264,128]{2,1,0:T(8,128)(2,1)S(1)} %pack.1.refs_1_), channel_id=1, source_target_pairs={{0,48},{16,64},{32,80},{48,96},{64,112},{80,0},{96,16},{112,32},{1... | collective-permute-start | bytes 202760 | tf_op jit(solution)/shard_map/ppermute | solution.py:319
  21.8 10.7 %collective-permute-start.11 = (bf16[1,264,128]{2,1,0:T(8,128)(2,1)S(1)}, bf16[1,264,128]{2,1,0:T(8,128)(2,1)S(1)}, u32[]{:S(2)}, u32[]{:S(2)}) collective-permute-start(bf16[1,264,128]{2,1,0:T(8,128)(2,1)S(1)} %pack.1.refs_1_), channel_id=1, source_target_pairs={{0,80},{16,96},{32,112},{48,0},{64,16},{80,32},{96,48},{112,64},{1... | collective-permute-start | bytes 202760 | tf_op jit(solution)/shard_map/ppermute | solution.py:319
  25.9 7.7 %collective-permute-start.13 = (bf16[1,264,128]{2,1,0:T(8,128)(2,1)S(1)}, bf16[1,264,128]{2,1,0:T(8,128)(2,1)S(1)}, u32[]{:S(2)}, u32[]{:S(2)}) collective-permute-start(bf16[1,264,128]{2,1,0:T(8,128)(2,1)S(1)} %pack.1.refs_1_), channel_id=1, source_target_pairs={{0,64},{16,80},{32,96},{48,112},{64,0},{80,16},{96,32},{112,48},{1... | collective-permute-start | bytes 202760 | tf_op jit(solution)/shard_map/ppermute | solution.py:319
  29.9 6.5 %collective-permute-start.2 = (bf16[1,264,128]{2,1,0:T(8,128)(2,1)S(1)}, bf16[1,264,128]{2,1,0:T(8,128)(2,1)S(1)}, u32[]{:S(2)}, u32[]{:S(2)}) collective-permute-start(bf16[1,264,128]{2,1,0:T(8,128)(2,1)S(1)} %collective-permute-done.1.refs_1_), channel_id=1, source_target_pairs={{0,1},{1,0},{2,3},{3,2},{4,5},{5,4},{6,7},{7,6},{8,9},{9,8},{10,11... | collective-permute-start | bytes 202760 | tf_op jit(solution)/shard_map/ppermute | solution.py:320
  32.0 4.4 %collective-permute-start.4 = (bf16[1,264,128]{2,1,0:T(8,128)(2,1)S(1)}, bf16[1,264,128]{2,1,0:T(8,128)(2,1)S(1)}, u32[]{:S(2)}, u32[]{:S(2)}) collective-permute-start(bf16[1,264,128]{2,1,0:T(8,128)(2,1)S(1)} %collective-permute-done.3.refs_3_), channel_id=1, source_target_pairs={{0,1},{1,0},{2,3},{3,2},{4,5},{5,4},{6,7},{7,6},{8,9},{9,8},{10,11... | collective-permute-start | bytes 202760 | tf_op jit(solution)/shard_map/ppermute | solution.py:320
  32.1 8.2 %collective-permute-start.6 = (bf16[1,264,128]{2,1,0:T(8,128)(2,1)S(1)}, bf16[1,264,128]{2,1,0:T(8,128)(2,1)S(1)}, u32[]{:S(2)}, u32[]{:S(2)}) collective-permute-start(bf16[1,264,128]{2,1,0:T(8,128)(2,1)S(1)} %collective-permute-done.5.refs_5_), channel_id=1, source_target_pairs={{0,1},{1,0},{2,3},{3,2},{4,5},{5,4},{6,7},{7,6},{8,9},{9,8},{10,11... | collective-permute-start | bytes 202760 | tf_op jit(solution)/shard_map/ppermute | solution.py:320
  32.5 7.7 %collective-permute-start.8 = (bf16[1,264,128]{2,1,0:T(8,128)(2,1)S(1)}, bf16[1,264,128]{2,1,0:T(8,128)(2,1)S(1)}, u32[]{:S(2)}, u32[]{:S(2)}) collective-permute-start(bf16[1,264,128]{2,1,0:T(8,128)(2,1)S(1)} %collective-permute-done.7.refs_7_), channel_id=1, source_target_pairs={{0,1},{1,0},{2,3},{3,2},{4,5},{5,4},{6,7},{7,6},{8,9},{9,8},{10,11... | collective-permute-start | bytes 202760 | tf_op jit(solution)/shard_map/ppermute | solution.py:320
  33.6 6.6 %collective-permute-start.10 = (bf16[1,264,128]{2,1,0:T(8,128)(2,1)S(1)}, bf16[1,264,128]{2,1,0:T(8,128)(2,1)S(1)}, u32[]{:S(2)}, u32[]{:S(2)}) collective-permute-start(bf16[1,264,128]{2,1,0:T(8,128)(2,1)S(1)} %collective-permute-done.9.refs_9_), channel_id=1, source_target_pairs={{0,1},{1,0},{2,3},{3,2},{4,5},{5,4},{6,7},{7,6},{8,9},{9,8},{10,11... | collective-permute-start | bytes 202760 | tf_op jit(solution)/shard_map/ppermute | solution.py:320
  36.4 3.8 %collective-permute-start.12 = (bf16[1,264,128]{2,1,0:T(8,128)(2,1)S(1)}, bf16[1,264,128]{2,1,0:T(8,128)(2,1)S(1)}, u32[]{:S(2)}, u32[]{:S(2)}) collective-permute-start(bf16[1,264,128]{2,1,0:T(8,128)(2,1)S(1)} %collective-permute-done.11.refs_11_), channel_id=1, source_target_pairs={{0,1},{1,0},{2,3},{3,2},{4,5},{5,4},{6,7},{7,6},{8,9},{9,8},{10,11... | collective-permute-start | bytes 202760 | tf_op jit(solution)/shard_map/ppermute | solution.py:320
  36.4 3.8 %collective-permute-start.14 = (bf16[1,264,128]{2,1,0:T(8,128)(2,1)S(1)}, bf16[1,264,128]{2,1,0:T(8,128)(2,1)S(1)}, u32[]{:S(2)}, u32[]{:S(2)}) collective-permute-start(bf16[1,264,128]{2,1,0:T(8,128)(2,1)S(1)} %collective-permute-done.13.refs_13_), channel_id=1, source_target_pairs={{0,1},{1,0},{2,3},{3,2},{4,5},{5,4},{6,7},{7,6},{8,9},{9,8},{10,11... | collective-permute-start | bytes 202760 | tf_op jit(solution)/shard_map/ppermute | solution.py:320
  40.3 34.4 %copy-start = (bf16[64,128]{1,0:T(8,128)(2,1)S(1)}, bf16[64,128]{1,0:T(8,128)(2,1)}, u32[]{:S(2)}) copy-start(bf16[64,128]{1,0:T(8,128)(2,1)} %x_ref.1) | copy-start | bytes 49156
  40.3 34.3 %copy-start.2 = (s32[128]{0:T(128)S(1)}, s32[128]{0:T(128)}, u32[]{:S(2)}) copy-start(s32[128]{0:T(128)} %param.8) | copy-start | bytes 1540
  40.3 38.9 %copy-start.3 = (f32[64,2000]{1,0:T(8,128)S(1)}, f32[64,2000]{1,0:T(8,128)}, u32[]{:S(2)}) copy-start(f32[64,2000]{1,0:T(8,128)} %param.9) | copy-start | bytes 1536004
  75.6 10.3 %all-to-all-start.2 = ((f32[16,8,256]{2,1,0:T(8,128)}), f32[16,8,256]{2,1,0:T(8,128)S(1)}, u32[]{:S(2)}, u32[]{:S(2)}) async-start(f32[16,8,256]{2,1,0:T(8,128)} %get-tuple-element.9), calls=%async_computation.2 | async-start | bytes 262144 | tf_op jit(solution)/shard_map/all_to_all | solution.py:299
  86.6 17.1 %all-to-all-start.3 = ((f32[16,8,256]{2,1,0:T(8,128)}), f32[16,8,256]{2,1,0:T(8,128)S(1)}, u32[]{:S(2)}, u32[]{:S(2)}) async-start(f32[16,8,256]{2,1,0:T(8,128)} %broadcast_in_dim.13), calls=%async_computation.3 | async-start | bytes 262144 | tf_op jit(solution)/shard_map/all_to_all | solution.py:299
  104.4 11.0 %all-to-all-start.4 = ((f32[16,8,256]{2,1,0:T(8,128)}), f32[16,8,256]{2,1,0:T(8,128)S(1)}, u32[]{:S(2)}, u32[]{:S(2)}) async-start(f32[16,8,256]{2,1,0:T(8,128)} %broadcast_in_dim.28), calls=%async_computation.4 | async-start | bytes 262144 | tf_op jit(solution)/shard_map/all_to_all | solution.py:299

commit v5 on v4

--- a/solution.py
+++ b/solution.py
@@ -23,9 +23,7 @@
 AXES = ("yl", "z", "yh", "x", "core")
 SIZES = (2, 8, 2, 4, 2)
 EARLY_GROUP = ("yl", "yh", "x")
-LATE_GROUP = ("z", "core")
-
-Z_STEPS = (1, 7, 2, 6, 3, 5, 4)
+PLANE = ("yl", "yh", "x", "core")
 
 
 def split3(v):
@@ -41,19 +39,21 @@
     return base
 
 
-def pack_kernel(late_ref, log_ref, out_ref):
+def pack_kernel(late_ref, log_ref, all_ref):
     cells = late_ref.shape[1]
     blocks = [late_ref[:, 128 * k : 128 * (k + 1)] for k in range(cells // 128)]
     logs = [log_ref[:, 128 * k : 128 * (k + 1)].astype(f32) for k in range(cells // 128)]
     tail = jnp.concatenate(logs + [jnp.zeros((8 - cells // 128, 128), f32)], 0).astype(bf16)
-    out_ref[0] = jnp.concatenate(blocks + [tail], 0)
-
-
-def pack(late, logs):
+    one = jnp.concatenate(blocks + [tail], 0)
+    for k in range(all_ref.shape[0]):
+        all_ref[k] = one
+
+
+def pack(late, logs, copies):
     rows = DIM * late.shape[1] // 128 + 8
     return pl.pallas_call(
         pack_kernel,
-        out_shape=jax.ShapeDtypeStruct((1, rows, 128), bf16),
+        out_shape=jax.ShapeDtypeStruct((copies, rows, 128), bf16),
         in_specs=[pl.BlockSpec(memory_space=pltpu.VMEM)] * 2,
         out_specs=pl.BlockSpec(memory_space=pltpu.VMEM),
         compiler_params=pltpu.CompilerParams(vmem_limit_bytes=8 * 2**20),
@@ -63,6 +63,7 @@
 
 def attention_kernel(*refs, n_x, n_late, tile, score_parts, parts, has_state):
     refs = list(refs)
+    slot_ref = refs.pop(0)
     x_refs = [refs.pop(0) for _ in range(n_x)]
     late_refs = [refs.pop(0) for _ in range(n_late)]
     if has_state:
@@ -75,7 +76,7 @@
     pairs = xa.shape[0]
     chunk = (late_refs[0].shape[1] - 8) * 2
     groups = chunk // 128
-    tiles = n_late * chunk // tile
+    tiles = n_late * late_refs[0].shape[0] * chunk // tile
 
     if not has_state:
         row = lax.broadcasted_iota(jnp.int32, (DIM, wide), 0)
@@ -107,7 +108,8 @@
         yw[:, pl.ds(first, chunk)] = jnp.concatenate([yb, ones.astype(bf16)], 0)
 
     for k, ref in enumerate(late_refs):
-        prepare_late(ref, 0, k)
+        for j in range(ref.shape[0]):
+            prepare_late(ref, j, k * ref.shape[0] + j)
     acc[...] = jnp.zeros_like(acc)
 
     def score_part(pair, first, offset, size, slot, top):
@@ -130,7 +132,7 @@
         following = jnp.minimum(n + 1, steps - 1)
         next_first = pl.multiple_of((following % tiles) * tile, tile)
         fresh = n % tiles == 0
-        left, right = 2 * pair, 2 * pair + 1
+        left, right = slot_ref[2 * pair], slot_ref[2 * pair + 1]
         carried = acc[...]
         if has_state:
             state = jnp.concatenate([state_ref[left], state_ref[right]], 1)
@@ -165,10 +167,10 @@
     lax.fori_loop(0, steps // 2, two_steps, jnp.full((1, wide), LOWEST, f32))
 
 
-def attention(early, late, state=None, tile=1024, score_parts=(512, 512), parts=(512, 512)):
+def attention(slots, early, late, state=None, tile=1024, score_parts=(512, 512), parts=(512, 512)):
     wide = 256
     pairs = early[0].shape[0] if state is not None else sum(e.shape[0] for e in early) // 2
-    late_total = len(late) * (late[0].shape[1] - 8) * 2
+    late_total = len(late) * late[0].shape[0] * (late[0].shape[1] - 8) * 2
     out_shape = [jax.ShapeDtypeStruct((2 * pairs, 72, 128), f32)]
     operands = list(early) + list(late)
     if state is None:
@@ -187,7 +189,7 @@
             has_state=state is not None,
         ),
         out_shape=out_shape,
-        in_specs=[vmem] * len(operands),
+        in_specs=[pl.BlockSpec(memory_space=pltpu.SMEM)] + [vmem] * len(operands),
         out_specs=[vmem] * len(out_shape),
         scratch_shapes=[
             pltpu.VMEM((late_total, 256), bf16),
@@ -197,7 +199,7 @@
             pltpu.VMEM((72, wide), f32),
         ],
         compiler_params=pltpu.CompilerParams(vmem_limit_bytes=32 * 2**20),
-    )(*operands)
+    )(slots, *operands)
 
 
 def moments_kernel(got_ref, x_ref, label_ref, projected_ref, sums_ref):
@@ -226,8 +228,10 @@
     lane = lax.broadcasted_iota(jnp.int32, (DIM, 128), 1)
     for q in range(FATES // DIM):
         second = jnp.where(lane == DIM + q, count[DIM * q : DIM * (q + 1)], second)
-    sums_ref[:8] = by_class.reshape(8, 8, FATES)
-    sums_ref[8:] = jnp.concatenate([second, jnp.zeros((DIM, 128), f32)], 1).reshape(8, 8, FATES)
+    sums_ref[:8] = by_class[:, :128].reshape(8, 8, 128)
+    sums_ref[8:16] = by_class[:, 128:].reshape(8, 8, 128)
+    sums_ref[16:24] = second.reshape(8, 8, 128)
+    sums_ref[24:] = jnp.zeros((8, 8, 128), f32)
 
 
 def moments(got, early, labels):
@@ -235,7 +239,7 @@
         moments_kernel,
         out_shape=(
             jax.ShapeDtypeStruct(early.shape, f32),
-            jax.ShapeDtypeStruct((16, 8, FATES), f32),
+            jax.ShapeDtypeStruct((32, 8, 128), f32),
         ),
         in_specs=[pl.BlockSpec(memory_space=pltpu.VMEM)] * 3,
         out_specs=(pl.BlockSpec(memory_space=pltpu.VMEM),) * 2,
@@ -246,8 +250,9 @@
 
 def correlate_kernel(sums_ref, split_ref, out_ref, right, stage, sems, *, cells, block):
     genes = split_ref.shape[0]
-    by_class = sums_ref[:8].reshape(DIM, FATES) / cells
-    second = sums_ref[8:].reshape(DIM, FATES)[:, :128]
+    halves = [sums_ref[8 * h : 8 * h + 8].reshape(DIM, 128) for h in range(3)]
+    by_class = jnp.concatenate(halves[:2], 1) / cells
+    second = halves[2]
     flipped = second.T
     share = jnp.concatenate([flipped[DIM + q : DIM + q + 1] for q in range(FATES // DIM)], 1) / cells
     mean = jnp.sum(by_class, 1, keepdims=True)
@@ -295,12 +300,17 @@
     return [(i, (i + k) % n) for i in range(n)]
 
 
+def shift_y(k):
+    place = [y % 2 * 2 + y // 2 for y in range(4)]
+    return [(place[y], place[(y + k) % 4]) for y in range(4)]
+
+
 def exchange(blocks, axes):
     return lax.all_to_all(blocks, axes, 0, 0, tiled=False)
 
 
-def spread(block, axes):
-    return exchange(jnp.broadcast_to(block[None], (16,) + block.shape), axes)
+def spread(block, axes, size):
+    return exchange(jnp.broadcast_to(block[None], (size,) + block.shape), axes)
 
 
 def program(early, late, late_logs, labels, loadings):
@@ -310,23 +320,25 @@
     low = turned - high
     split = jnp.concatenate([high, low, high, low], 1).astype(bf16)
 
-    early_all = spread(early, EARLY_GROUP)
-    late_one = pack(late, late_logs)
-    swap = [(0, 1), (1, 0)]
-    late_near = lax.ppermute(late_one, "core", swap)
-    late_far = []
-    for k in Z_STEPS:
-        own = lax.ppermute(late_one, "z", shift(SIZES[1], k))
-        late_far += [own, lax.ppermute(own, "core", swap)]
-    partial, prepared = attention([early_all], [late_one, late_near])
-    (partial,) = attention(
-        [prepared], late_far, partial, tile=3584, score_parts=(512,) * 7, parts=(512,) * 7
+    late_copies = pack(late, late_logs, SIZES[1])
+    late_own = exchange(late_copies, "z")
+    late_other = lax.ppermute(late_own, "core", [(0, 1), (1, 0)])
+    line = [early] + [lax.ppermute(early, "x", shift(4, k)) for k in range(1, 4)]
+    line = jnp.stack(line)
+    turns = [lax.ppermute(line, ("yl", "yh"), shift_y(k)) for k in range(1, 4)]
+    y, x = 2 * lax.axis_index("yh") + lax.axis_index("yl"), lax.axis_index("x")
+    back = jnp.arange(16, dtype=jnp.int32)
+    to_y, to_x = (y - back // 4) % 4, (x - back % 4) % 4
+    slots = (to_y % 2 * 8 + to_y // 2 * 4 + to_x).astype(jnp.int32)
+    parts = (512,) * 8
+    partial, _ = attention(
+        slots, [line] + turns, [late_own, late_other], tile=4096, score_parts=parts, parts=parts
     )
     got = exchange(partial, EARLY_GROUP)
     projected, sums = moments(got, early, labels[None])
-    sums = jnp.sum(exchange(sums, EARLY_GROUP), 0)
-    sums = jnp.sum(spread(sums, LATE_GROUP), 0)
-    sums = spread(sums, EARLY_GROUP)
+    sums = jnp.sum(exchange(sums, PLANE), 0)
+    sums = jnp.sum(spread(sums, "z", SIZES[1]), 0)
+    sums = spread(sums, PLANE, 32)
     return projected, correlate(sums, split, cells)
 
 

time: 118 us -> 123 us (1.042)
  blocking collectives: 18.2 us -> 39 us
  starting transfers between devices: 48.5 us -> 28.3 us
  waiting for transfers between devices: 22 us -> 26.7 us
  local copies, waits for them, and re-layouts: 4.67 us -> 3.15 us
    all_to_all x1 -> x2, blocking collectives: 18.2 us -> 39 us  [exchange(): return lax.all_to_all(blocks, axes, 0, 0, tiled=False)]
    ppermute x15 -> x7, starting transfers between devices: 25.7 us -> 11.7 us  [the longest x3 5.42 us: program(): lax.ppermute(early, 'x', shift(4, k))]
    all_to_all x4 -> x3, starting transfers between devices: 22.8 us -> 16.6 us  [exchange(): return lax.all_to_all(blocks, axes, 0, 0, tiled=False)]
    ppermute x15 -> x7, waiting for transfers between devices: 0.04 us -> 5.6 us  [the longest x3 4.26 us: program(): turns = [lax.ppermute(line, ('yl', 'yh'), shift_y(k)) for k in range(1, 4)]]
    broadcast_in_dim x3 -> x2, local copies, waits for them, and re-layouts: 2.8 us -> 1.29 us  [spread(): return exchange(jnp.broadcast_to(block[None], (size,) + block.shape), axes)]
    all_to_all x4 -> x3, waiting for transfers between devices: 21.9 us -> 21.1 us  [exchange(): return lax.all_to_all(blocks, axes, 0, 0, tiled=False)]
    pallas_call x2 -> x1, Pallas kernels: 19.4 us -> 19.7 us  [attention(): pl.pallas_call(functools.partial(attention_kernel, n_x=len(early), n_late...]
  transfers between devices with their start and end apart: 19 -> 10, of which waited for: 3 -> 7; matrix products, arithmetic and copies ran while one was open for 2% -> 2% of each run, Pallas kernels for 3% -> 0%
where the time goes in v5:
time: 123 us; the launch traced here: 122 us
  blocking collectives  39 us (32%)
  starting transfers between devices  28.3 us (23%)
  waiting for transfers between devices  26.7 us (22%)
  Pallas kernels  22.7 us (18%)
  local copies, waits for them, and re-layouts  3.15 us (3%)
  other arithmetic  1.67 us (1%)
    all_to_all x2, blocking collectives, exchange(): return lax.all_to_all(blocks, axes, 0, 0, tiled=False)  39 us
    all_to_all x3, waiting for transfers between devices, exchange(): return lax.all_to_all(blocks, axes, 0, 0, tiled=False)  21.1 us
    pallas_call x1, Pallas kernels, attention(): pl.pallas_call(functools.partial(attention_kernel, n_x=len(early), n_late...  19.7 us
    all_to_all x3, starting transfers between devices, exchange(): return lax.all_to_all(blocks, axes, 0, 0, tiled=False)  16.6 us
    ppermute x3, starting transfers between devices, program(): lax.ppermute(early, 'x', shift(4, k))  5.42 us
    ppermute x3, waiting for transfers between devices, program(): turns = [lax.ppermute(line, ('yl', 'yh'), shift_y(k)) for k in range(1, 4)]  4.26 us
    ppermute x3, starting transfers between devices, program(): turns = [lax.ppermute(line, ('yl', 'yh'), shift_y(k)) for k in range(1, 4)]  3.85 us
  transfers between devices with their start and end apart: 10, of which 7 were waited for; matrix products, arithmetic and copies ran while one was open for 2% of the time, Pallas kernels for 0%

profile of v5, /device:TPU:1, one launch (start us, length us, event | category | flops | bytes accessed | tf_op | source)
XLA Modules:
  0.0 122.2 jit_solution(4166982502290590032)
XLA Ops:
  0.6 0.7 broadcast_in_dim.8.log_ref
  1.3 0.8 copy-done
  2.2 25.1 %all_to_all.25.refs_5_ = bf16[8,264,128]{2,1,0:T(8,128)(2,1)S(1)} all-to-all(bf16[8,264,128]{2,1,0:T(8,128)(2,1)S(1)} %pack.1), channel_id=1, replica_groups=mesh['yl'=2,'z'=8,'yh'=2,'x'=4,'core'=2] {'z'}, dimensions={0} | all-to-all | bytes 1081344 | tf_op jit(solution)/shard_map/all_to_all | solution.py:309
  27.4 2.5 %collective-permute-start.6 = (bf16[8,264,128]{2,1,0:T(8,128)(2,1)S(1)}, bf16[8,264,128]{2,1,0:T(8,128)(2,1)S(1)}, u32[]{:S(2)}, u32[]{:S(2)}) collective-permute-start(bf16[8,264,128]{2,1,0:T(8,128)(2,1)S(1)} %all_to_all.25.refs_5_), channel_id=1, source_target_pairs={{0,1},{1,0},{2,3},{3,2},{4,5},{5,4},{6,7},{7,6},{8,9},{9,8},{10,11... | collective-permute-start | bytes 1622024 | tf_op jit(solution)/shard_map/ppermute | solution.py:325
  29.8 2.7 %collective-permute-start.1 = (bf16[64,128]{1,0:T(8,128)(2,1)}, bf16[64,128]{1,0:T(8,128)(2,1)S(1)}, u32[]{:S(2)}, u32[]{:S(2)}) collective-permute-start(bf16[64,128]{1,0:T(8,128)(2,1)} %x_ref.1), channel_id=1, source_target_pairs={{0,4},{2,6},{4,0},{6,2},{1,5},{3,7},{5,1},{7,3},{8,12},{10,14},{12... | collective-permute-start | bytes 49160 | tf_op jit(solution)/shard_map/ppermute | solution.py:326
  32.9 2.4 %collective-permute-start.2 = (bf16[64,128]{1,0:T(8,128)(2,1)}, bf16[64,128]{1,0:T(8,128)(2,1)S(1)}, u32[]{:S(2)}, u32[]{:S(2)}) collective-permute-start(bf16[64,128]{1,0:T(8,128)(2,1)} %x_ref.1), channel_id=1, source_target_pairs={{0,6},{2,0},{4,2},{6,4},{1,7},{3,1},{5,3},{7,5},{8,14},{10,8},{12,... | collective-permute-start | bytes 49160 | tf_op jit(solution)/shard_map/ppermute | solution.py:326
  35.3 1.3 %collective-permute-done = bf16[64,128]{1,0:T(8,128)(2,1)S(1)} collective-permute-done((bf16[64,128]{1,0:T(8,128)(2,1)}, bf16[64,128]{1,0:T(8,128)(2,1)S(1)}, u32[]{:S(2)}, u32[]{:S(2)}) %collective-permute-start) | collective-permute-done | bytes 16416 | tf_op jit(solution)/shard_map/ppermute | solution.py:326
  36.6 0.7 pad_maximum_fusion.1.refs_1_
  37.3 2.8 %collective-permute-start.5 = (bf16[4,64,128]{2,1,0:T(8,128)(2,1)S(1)}, bf16[4,64,128]{2,1,0:T(8,128)(2,1)S(1)}, u32[]{:S(2)}, u32[]{:S(2)}) collective-permute-start(bf16[4,64,128]{2,1,0:T(8,128)(2,1)S(1)} %pad_maximum_fusion.1.refs_1_), channel_id=1, source_target_pairs={{0,136},{128,0},{8,128},{136,8},{1,137},{129,1},{9,129},{137,9},{2... | collective-permute-start | bytes 196616 | tf_op jit(solution)/shard_map/ppermute | solution.py:328
  40.5 0.7 collective-permute-start.3
  41.5 3.4 %collective-permute-done.4.refs_3_ = bf16[4,64,128]{2,1,0:T(8,128)(2,1)S(1)} collective-permute-done((bf16[4,64,128]{2,1,0:T(8,128)(2,1)S(1)}, bf16[4,64,128]{2,1,0:T(8,128)(2,1)S(1)}, u32[]{:S(2)}, u32[]{:S(2)}) %collective-permute-start.4) | collective-permute-done | bytes 65568 | tf_op jit(solution)/shard_map/ppermute | solution.py:328
  44.8 0.6 collective-permute-done.3.refs_2_
  45.5 19.7 %shard_map.68 = (f32[16,72,128]{2,1,0:T(8,128)S(1)}, bf16[8,256,256]{2,1,0:T(8,128)(2,1)}) custom-call(s32[16]{0:T(128)S(1)} %fusion.2.refs_0_, bf16[4,64,128]{2,1,0:T(8,128)(2,1)S(1)} %pad_maximum_fusion.1.refs_1_, bf16[4,64,128]{2,1,0:T(8,128)(2,1)S(1)} %collective-permute-done.3.refs_2_, bf16[4,64,128]{2,1,0:T(8,128)(2,1)S(1)} %collective-permute-done.4.refs_3_, ...), custom_call_target="tpu_custom_call" | custom-call | tf_op jit(solution)/shard_map/pallas_call | solution.py:181
  65.2 13.8 %all_to_all.26.got_ref = f32[16,72,128]{2,1,0:T(8,128)S(1)} all-to-all(f32[16,72,128]{2,1,0:T(8,128)S(1)} %get-tuple-element.5), channel_id=1, replica_groups=mesh['yl'=2,'z'=8,'yh'=2,'x'=4,'core'=2] {'yl','yh','x'}, dimensions={0} | all-to-all | bytes 1179648 | tf_op jit(solution)/shard_map/all_to_all | solution.py:309
  79.0 1.0 moments.1
  80.0 8.2 %all-to-all-start.2 = ((f32[32,8,128]{2,1,0:T(8,128)}), f32[32,8,128]{2,1,0:T(8,128)S(1)}, u32[]{:S(2)}, u32[]{:S(2)}) async-start(f32[32,8,128]{2,1,0:T(8,128)} %get-tuple-element.7), calls=%async_computation.2 | async-start | bytes 262144 | tf_op jit(solution)/shard_map/all_to_all | solution.py:309
  88.6 7.4 %all-to-all-done.2 = f32[32,8,128]{2,1,0:T(8,128)S(1)} async-done(((f32[32,8,128]{2,1,0:T(8,128)}), f32[32,8,128]{2,1,0:T(8,128)S(1)}, u32[]{:S(2)}, u32[]{:S(2)}) %all-to-all-start.2) | async-done | bytes 131104 | tf_op jit(solution)/shard_map/all_to_all | solution.py:309
  96.6 3.3 %all-to-all-start.3 = ((f32[8,8,128]{2,1,0:T(8,128)}), f32[8,8,128]{2,1,0:T(8,128)S(1)}, u32[]{:S(2)}, u32[]{:S(2)}) async-start(f32[8,8,128]{2,1,0:T(8,128)} %broadcast_in_dim.20), calls=%async_computation.3 | async-start | bytes 65536 | tf_op jit(solution)/shard_map/all_to_all | solution.py:309
  100.2 6.6 %all-to-all-done.3 = f32[8,8,128]{2,1,0:T(8,128)S(1)} async-done(((f32[8,8,128]{2,1,0:T(8,128)}), f32[8,8,128]{2,1,0:T(8,128)S(1)}, u32[]{:S(2)}, u32[]{:S(2)}) %all-to-all-start.3) | async-done | bytes 32800 | tf_op jit(solution)/shard_map/all_to_all | solution.py:309
  106.8 0.7 broadcast_in_dim.21
  107.5 5.0 %all-to-all-start.4 = ((f32[32,8,128]{2,1,0:T(8,128)}), f32[32,8,128]{2,1,0:T(8,128)S(1)}, u32[]{:S(2)}, u32[]{:S(2)}) async-start(f32[32,8,128]{2,1,0:T(8,128)} %broadcast_in_dim.21), calls=%async_computation.4 | async-start | bytes 262144 | tf_op jit(solution)/shard_map/all_to_all | solution.py:309
  112.5 0.7 pad_maximum_fusion.split_ref
  113.2 7.0 %all-to-all-done.4.sums_ref = f32[32,8,128]{2,1,0:T(8,128)S(1)} async-done(((f32[32,8,128]{2,1,0:T(8,128)}), f32[32,8,128]{2,1,0:T(8,128)S(1)}, u32[]{:S(2)}, u32[]{:S(2)}) %all-to-all-start.4) | async-done | bytes 131104 | tf_op jit(solution)/shard_map/all_to_all | solution.py:309
  120.3 1.9 %correlate.1 = f32[2000,256]{1,0:T(8,128)} custom-call(f32[32,8,128]{2,1,0:T(8,128)S(1)} %all-to-all-done.4.sums_ref, bf16[2000,256]{1,0:T(8,128)(2,1)S(1)} %pad_maximum_fusion.split_ref), custom_call_target="tpu_custom_call" | custom-call | tf_op jit(solution)/shard_map/correlate/pallas_call | solution.py:284
  (20 shorter events, 2.2 us)
Async XLA Ops:
  1.3 0.8 copy-start
  2.2 76.8 %copy-start.1 = (bf16[64,128]{1,0:T(8,128)(2,1)S(1)}, bf16[64,128]{1,0:T(8,128)(2,1)}, u32[]{:S(2)}) copy-start(bf16[64,128]{1,0:T(8,128)(2,1)} %x_ref.1) | copy-start | bytes 49156
  2.2 76.8 %copy-start.2 = (s32[128]{0:T(128)S(1)}, s32[128]{0:T(128)}, u32[]{:S(2)}) copy-start(s32[128]{0:T(128)} %param.8) | copy-start | bytes 1540
  27.4 60.9 %copy-start.3 = (f32[64,2000]{1,0:T(8,128)S(1)}, f32[64,2000]{1,0:T(8,128)}, u32[]{:S(2)}) copy-start(f32[64,2000]{1,0:T(8,128)} %param.9) | copy-start | bytes 1536004
  27.4 18.1 %collective-permute-start.6 = (bf16[8,264,128]{2,1,0:T(8,128)(2,1)S(1)}, bf16[8,264,128]{2,1,0:T(8,128)(2,1)S(1)}, u32[]{:S(2)}, u32[]{:S(2)}) collective-permute-start(bf16[8,264,128]{2,1,0:T(8,128)(2,1)S(1)} %all_to_all.25.refs_5_), channel_id=1, source_target_pairs={{0,1},{1,0},{2,3},{3,2},{4,5},{5,4},{6,7},{7,6},{8,9},{9,8},{10,11... | collective-permute-start | bytes 1622024 | tf_op jit(solution)/shard_map/ppermute | solution.py:325
  29.8 5.4 %collective-permute-start.1 = (bf16[64,128]{1,0:T(8,128)(2,1)}, bf16[64,128]{1,0:T(8,128)(2,1)S(1)}, u32[]{:S(2)}, u32[]{:S(2)}) collective-permute-start(bf16[64,128]{1,0:T(8,128)(2,1)} %x_ref.1), channel_id=1, source_target_pairs={{0,4},{2,6},{4,0},{6,2},{1,5},{3,7},{5,1},{7,3},{8,12},{10,14},{12... | collective-permute-start | bytes 49160 | tf_op jit(solution)/shard_map/ppermute | solution.py:326
  32.6 4.0 %collective-permute-start = (bf16[64,128]{1,0:T(8,128)(2,1)}, bf16[64,128]{1,0:T(8,128)(2,1)S(1)}, u32[]{:S(2)}, u32[]{:S(2)}) collective-permute-start(bf16[64,128]{1,0:T(8,128)(2,1)} %x_ref.1), channel_id=1, source_target_pairs={{0,2},{2,4},{4,6},{6,0},{1,3},{3,5},{5,7},{7,1},{8,10},{10,12},{12... | collective-permute-start | bytes 49160 | tf_op jit(solution)/shard_map/ppermute | solution.py:326
  32.9 3.7 %collective-permute-start.2 = (bf16[64,128]{1,0:T(8,128)(2,1)}, bf16[64,128]{1,0:T(8,128)(2,1)S(1)}, u32[]{:S(2)}, u32[]{:S(2)}) collective-permute-start(bf16[64,128]{1,0:T(8,128)(2,1)} %x_ref.1), channel_id=1, source_target_pairs={{0,6},{2,0},{4,2},{6,4},{1,7},{3,1},{5,3},{7,5},{8,14},{10,8},{12,... | collective-permute-start | bytes 49160 | tf_op jit(solution)/shard_map/ppermute | solution.py:326
  37.3 4.1 %collective-permute-start.5 = (bf16[4,64,128]{2,1,0:T(8,128)(2,1)S(1)}, bf16[4,64,128]{2,1,0:T(8,128)(2,1)S(1)}, u32[]{:S(2)}, u32[]{:S(2)}) collective-permute-start(bf16[4,64,128]{2,1,0:T(8,128)(2,1)S(1)} %pad_maximum_fusion.1.refs_1_), channel_id=1, source_target_pairs={{0,136},{128,0},{8,128},{136,8},{1,137},{129,1},{9,129},{137,9},{2... | collective-permute-start | bytes 196616 | tf_op jit(solution)/shard_map/ppermute | solution.py:328
  40.1 4.7 %collective-permute-start.4 = (bf16[4,64,128]{2,1,0:T(8,128)(2,1)S(1)}, bf16[4,64,128]{2,1,0:T(8,128)(2,1)S(1)}, u32[]{:S(2)}, u32[]{:S(2)}) collective-permute-start(bf16[4,64,128]{2,1,0:T(8,128)(2,1)S(1)} %pad_maximum_fusion.1.refs_1_), channel_id=1, source_target_pairs={{0,8},{128,136},{8,0},{136,128},{1,9},{129,137},{9,1},{137,129},{2... | collective-permute-start | bytes 196616 | tf_op jit(solution)/shard_map/ppermute | solution.py:328
  40.5 5.0 %collective-permute-start.3 = (bf16[4,64,128]{2,1,0:T(8,128)(2,1)S(1)}, bf16[4,64,128]{2,1,0:T(8,128)(2,1)S(1)}, u32[]{:S(2)}, u32[]{:S(2)}) collective-permute-start(bf16[4,64,128]{2,1,0:T(8,128)(2,1)S(1)} %pad_maximum_fusion.1.refs_1_), channel_id=1, source_target_pairs={{0,128},{128,8},{8,136},{136,0},{1,129},{129,9},{9,137},{137,1},{2... | collective-permute-start | bytes 196616 | tf_op jit(solution)/shard_map/ppermute | solution.py:328
  80.0 16.0 %all-to-all-start.2 = ((f32[32,8,128]{2,1,0:T(8,128)}), f32[32,8,128]{2,1,0:T(8,128)S(1)}, u32[]{:S(2)}, u32[]{:S(2)}) async-start(f32[32,8,128]{2,1,0:T(8,128)} %get-tuple-element.7), calls=%async_computation.2 | async-start | bytes 262144 | tf_op jit(solution)/shard_map/all_to_all | solution.py:309
  96.6 10.1 %all-to-all-start.3 = ((f32[8,8,128]{2,1,0:T(8,128)}), f32[8,8,128]{2,1,0:T(8,128)S(1)}, u32[]{:S(2)}, u32[]{:S(2)}) async-start(f32[8,8,128]{2,1,0:T(8,128)} %broadcast_in_dim.20), calls=%async_computation.3 | async-start | bytes 65536 | tf_op jit(solution)/shard_map/all_to_all | solution.py:309
  107.5 12.8 %all-to-all-start.4 = ((f32[32,8,128]{2,1,0:T(8,128)}), f32[32,8,128]{2,1,0:T(8,128)S(1)}, u32[]{:S(2)}, u32[]{:S(2)}) async-start(f32[32,8,128]{2,1,0:T(8,128)} %broadcast_in_dim.21), calls=%async_computation.4 | async-start | bytes 262144 | tf_op jit(solution)/shard_map/all_to_all | solution.py:309
